TPU v7x, 32 devices: a whole 2x2x4 slice. The times are simulated.
32 devices in a mesh: leaf: 8 (over z, y), chol: 4 (over x, core).
Axes of the slice: x: 2, y: 2, z: 4, core: 2. Of those that a mesh axis runs over, the one named last changes fastest.
Arguments:
- coords: float32 [3, 3072], P(None, 'leaf'), may hold values from 0 to 1
- observed: float32 [16, 3072], P(None, 'leaf'), may hold values from -6 to 6
- cond_index: int32 [8, 512], P('leaf'), may hold values from 0 to 2687, as said below
Outputs:
- cond_mean: float32 [16, 3072], P(None, ('leaf', 'chol'))
- whitened: float32 [16, 3072], P(None, ('leaf', 'chol'))
Inputs may be any that keep to these rules, and one draw needn't show every extreme that they name: `cond_index`: slot s of a leaf lies in group s // 128. A group names 128 distinct sites of one leaf. Different groups of a leaf name different leaves, all earlier than the leaf, except groups that name sites of the leaf itself. Every leaf numbered 4 or more names 4 earlier leaves; leaf b below that names b earlier leaves.
All inputs are finite; a program needn't handle non-finite values.
Results may differ from a plain program's by a relative error of at most 0.0003.
Values sent between devices are 32-bit elements; how exact they have to be, the bound alone decides.
No kernel may reach another device: no remote copies, remote signals or barrier semaphores. Data moves between devices by JAX's collectives and lax.ppermute only.
A program may use at most 128 MiB of HBM per device.

v0:
```python
import functools
import jax
import jax.numpy as jnp
from jax import lax
from jax.experimental import pallas as pl
from jax.experimental.pallas import tpu as pltpu
from jax.sharding import PartitionSpec as P

length_scale = 0.3
nugget = 0.2
B = 128
G = 16
LANES = 128
f32 = jnp.float32
bf16 = jnp.bfloat16


def pieces(x):
    high = x.astype(bf16)
    rest = x - high.astype(f32)
    mid = rest.astype(bf16)
    low = (rest - mid.astype(f32)).astype(bf16)
    return high, mid, low


def kernel(leaf_axis, chol_axis, got_ref, own_ref, idx_ref, mean_ref, white_ref,
           a_ref, d_ref, v_ref, r_ref, w_ref, panel_ref, z_ref, m_ref):
    own = own_ref.shape[1]
    cond = got_ref.shape[1]
    cols = own_ref.shape[0] - 3
    total = cond + own
    nblk = total // B
    nc = cond // B
    leaf_id = lax.axis_index(leaf_axis)
    chol_id = lax.axis_index(chol_axis)

    lane = lax.broadcasted_iota(jnp.int32, (B, B), 1)
    sub = lax.broadcasted_iota(jnp.int32, (B, B), 0)

    row_form, col_form = [], []
    for k in range(nblk):
        if k < nc:
            blk = got_ref[:, k * B:(k + 1) * B]
            alive = (idx_ref[:, k * B:(k + 1) * B] // own != leaf_id).astype(f32)
            vals = blk[3:] * alive
            vals2 = vals
        else:
            blk = own_ref[:, (k - nc) * B:(k - nc + 1) * B]
            alive = jnp.ones((1, B), f32)
            vals = blk[3:]
            vals2 = jnp.zeros_like(vals)
        stack = jnp.concatenate(
            [vals, vals2, blk[:3], alive, jnp.zeros((B - 2 * cols - 4, B), f32)], axis=0)
        t = stack.T
        row_form.append((blk[0:1], blk[1:2], blk[2:3], alive))
        c0 = 2 * cols
        col_form.append(tuple(jnp.broadcast_to(t[:, c0 + i:c0 + i + 1], (B, B)) for i in range(4)))
        a_ref[k * B:(k + 1) * B, total:total + B] = jnp.where(lane < c0, t, 0.0)

    for k in range(nblk):
        cx, cy, cz, ca = col_form[k]
        for c in range(nblk):
            if c < k:
                a_ref[k * B:(k + 1) * B, c * B:(c + 1) * B] = jnp.zeros((B, B), f32)
                continue
            rx, ry, rz, ra = row_form[c]
            dx, dy, dz = cx - rx, cy - ry, cz - rz
            sq = jnp.maximum(dx * dx + dy * dy + dz * dz, 1e-30)
            dist = sq * lax.rsqrt(sq)
            kern = jnp.exp(dist * (-1.0 / length_scale)) * (ca * ra)
            if c == k:
                kern = jnp.where(lane == sub, kern + (nugget * ra + 1.0 - ra), kern)
            a_ref[k * B:(k + 1) * B, c * B:(c + 1) * B] = kern

    lane8 = lax.broadcasted_iota(jnp.int32, (8, B), 1)
    lanec = lax.broadcasted_iota(jnp.int32, (1, B), 1)

    def block_step(k, carry):
        row0 = pl.multiple_of(k * B, B)
        d_ref[...] = a_ref[pl.ds(row0, B), pl.ds(row0, B)]
        for s in range(B // G):
            base = s * G
            halves = G // 8
            for h in range(halves):
                p = d_ref[base + 8 * h:base + 8 * h + 8, :]
                for c in range(8 * h + 8):
                    v_ref[h, c] = jnp.broadcast_to(p[:, base + c:base + c + 1], (8, B))
            S = [[None] * G for _ in range(G)]
            for i in range(G):
                for c in range(i + 1):
                    S[i][c] = jnp.broadcast_to(v_ref[i // 8, c, i % 8:i % 8 + 1, :], (8, B))
            R = [None] * G
            rs = [None] * G
            for i in range(G):
                row = jnp.broadcast_to(d_ref[base + i:base + i + 1, :], (8, B))
                R[i] = jnp.where((lane8 >= base) & (lane8 < base + G),
                                 (lane8 == base + i).astype(f32), row)
            for j in range(G):
                rs[j] = lax.rsqrt(S[j][j])
                R[j] = R[j] * rs[j]
                for i in range(j + 1, G):
                    S[i][j] = S[i][j] * rs[j]
                for i in range(j + 1, G):
                    for c in range(j + 1, i + 1):
                        S[i][c] = S[i][c] - S[i][j] * S[c][j]
                for i in range(j + 1, G):
                    R[i] = R[i] - S[i][j] * R[j]
            for i in range(G):
                r_ref[i:i + 1, :] = R[i][0:1, :]
            rr = r_ref[...]
            w_ref[base:base + G, :] = jnp.where(lanec < base + G, rr, 0.0)
            if s + 1 < B // G:
                h, m, l = pieces(rr)
                left = jnp.concatenate([h, h, m, m, h, l], axis=0)
                right = jnp.concatenate([h, m, h, m, l, h], axis=0)
                upd = lax.dot_general(left[:, base + G:] if False else left, right, (((0,), (0,)), ((), ())),
                                      preferred_element_type=f32)
                keep = (lanec < base) | (lanec >= base + G)
                old = d_ref[base + G:, :]
                d_ref[base + G:, :] = jnp.where(keep, old, 0.0) - upd[base + G:, :]
        panel = jnp.dot(w_ref[...], a_ref[pl.ds(row0, B), :], precision=lax.Precision.HIGHEST,
                        preferred_element_type=f32)
        panel_ref[...] = panel
        panel_ref[:, pl.ds(row0, B)] = jnp.zeros((B, B), f32)
        z_ref[pl.ds(row0, B), :] = panel[:, total:]

        def row_update(j, c):
            r0 = pl.multiple_of(j * B, B)
            upd = lax.dot_general(panel_ref[:, pl.ds(r0, B)], panel_ref[...], (((0,), (0,)), ((), ())),
                                  precision=lax.Precision.HIGHEST, preferred_element_type=f32)
            a_ref[pl.ds(r0, B), :] = a_ref[pl.ds(r0, B), :] - upd
            return c
        lax.fori_loop(k + 1, nblk, row_update, 0)

        @pl.when(k == nc - 1)
        def _():
            m_ref[...] = -a_ref[cond:, total:total + B]
        return carry

    lax.fori_loop(0, nblk, block_step, 0)
    out = mean_ref.shape[1]
    start = pl.multiple_of(chol_id * out, 8)
    pad = jnp.zeros((B - out, B), f32)
    mt = jnp.concatenate([m_ref[pl.ds(start, out), :], pad], axis=0).T
    zt = jnp.concatenate([z_ref[pl.ds(cond + start, out), :], pad], axis=0).T
    mean_ref[...] = mt[cols:2 * cols, :out]
    white_ref[...] = zt[:cols, :out]


def on_device(leaves, chols, coords, observed, cond_index):
    leaf_id = lax.axis_index("leaf")
    own = coords.shape[1]
    cond = cond_index.shape[1]
    cols = observed.shape[0]
    packed = jnp.concatenate([coords, observed], axis=0)
    every = lax.all_gather(packed, "leaf", axis=1, tiled=True)
    got = jnp.take(every, cond_index[0], axis=1)
    out = own // chols
    total = own + cond
    return pl.pallas_call(
        functools.partial(kernel, "leaf", "chol"),
        out_shape=(jax.ShapeDtypeStruct((cols, out), f32),) * 2,
        in_specs=[pl.BlockSpec(memory_space=pltpu.VMEM)] * 3,
        out_specs=(pl.BlockSpec(memory_space=pltpu.VMEM),) * 2,
        scratch_shapes=[
            pltpu.VMEM((total, total + B), f32),
            pltpu.VMEM((B, B), f32),
            pltpu.VMEM((G // 8, G, 8, B), f32),
            pltpu.VMEM((G, B), f32),
            pltpu.VMEM((B, B), f32),
            pltpu.VMEM((B, total + B), f32),
            pltpu.VMEM((total, B), f32),
            pltpu.VMEM((own, B), f32),
        ],
        compiler_params=pltpu.CompilerParams(vmem_limit_bytes=48 << 20),
        name="vecchia",
    )(got, packed, cond_index)


def solution(mesh):
    return jax.shard_map(
        functools.partial(on_device, mesh.shape["leaf"], mesh.shape["chol"]),
        mesh=mesh,
        in_specs=(P(None, "leaf"), P(None, "leaf"), P("leaf", None)),
        out_specs=(P(None, ("leaf", "chol")), P(None, ("leaf", "chol"))),
        check_vma=False,
    )
```

profile of v0, /device:TPU:0, one launch (start us, length us, event | category | flops | bytes accessed | tf_op | source)
XLA Modules:
  0.0 84.5 jit_solution(6522751449745792149)
XLA Ops:
  0.6 0.0 copy-start
  0.6 0.8 pad_maximum_fusion.own_ref
  1.4 32.6 %all_gather.3 = f32[19,3072]{1,0:T(8,128)S(1)} all-gather(f32[19,384]{1,0:T(8,128)S(1)} %pad_maximum_fusion.own_ref), channel_id=1, replica_groups=mesh['leaf'=8,'chol'=4] {'leaf'}, dimensions={1}, use_global_device_ids=true | all-gather | bytes 262656 | tf_op jit(solution)/shard_map/all_gather | solution.py:156
  34.0 0.5 copy.7
  34.5 0.0 copy-done
  34.5 1.0 %gather_fusion = f32[512,19]{1,0:T(8,128)S(1)} fusion(f32[19,3072]{0,1:T(8,128)S(1)} %copy.7, s32[1024]{0:T(1024)S(1)} %pad_clamp_fusion), kind=kCustom, calls=%fused_computation | custom fusion | bytes 79872 | tf_op jit(solution)/shard_map/jit(_take)/gather | solution.py:157
  35.6 0.1 copy.8
  35.7 48.7 %vecchia.1 = (f32[16,96]{1,0:T(8,128)}, f32[16,96]{1,0:T(8,128)}) custom-call(f32[19,512]{1,0:T(8,128)S(1)} %select_bitcast_fusion.got_ref, f32[19,384]{1,0:T(8,128)S(1)} %pad_maximum_fusion.own_ref, s32[1,512]{1,0:T(1,128)S(1)} %copy-done), custom_call_target="tpu_custom_call" | custom-call | tf_op jit(solution)/shard_map/vecchia/pallas_call | solution.py:160
  (4 shorter events, 0.0 us)
Async XLA Ops:
  0.6 33.9 %copy-start = (s32[1,512]{1,0:T(1,128)S(1)}, s32[1,512]{1,0:T(1,128)}, u32[]{:S(2)}) copy-start(s32[1,512]{1,0:T(1,128)} %idx_ref.1) | copy-start | bytes 6148
where the time goes:
time: 84.7 us; the launch traced here: 84.5 us
  Pallas kernels  48.7 us (57%)
  blocking collectives  32.6 us (38%)
  local copies, waits for them, and re-layouts  1.65 us (2%)
    pallas_call x1, Pallas kernels, on_device(): pl.pallas_call(functools.partial(kernel, 'leaf', 'chol'), out_shape=(jax....  48.7 us
    all_gather x1, blocking collectives, on_device(): every = lax.all_gather(packed, 'leaf', axis=1, tiled=True)  32.6 us

commit v1 on v0

v1 whole, which is shorter than its diff:
```python
import functools
import jax
import jax.numpy as jnp
from jax import lax
from jax.experimental import pallas as pl
from jax.experimental.pallas import tpu as pltpu
from jax.sharding import PartitionSpec as P

length_scale = 0.3
nugget = 0.2
B = 128
G = 16
LANES = 128
f32 = jnp.float32
bf16 = jnp.bfloat16


def halves(x):
    high = x.astype(bf16)
    return high, (x - high.astype(f32)).astype(bf16)


def kernel(leaf_axis, chol_axis, got_ref, own_ref, idx_ref, mean_ref, white_ref,
           a_ref, d_ref, v_ref, x_ref, w_ref, z_ref, m_ref):
    own = own_ref.shape[1]
    cond = got_ref.shape[1]
    cols = own_ref.shape[0] - 3
    total = cond + own
    nblk = total // B
    nc = cond // B
    leaf_id = lax.axis_index(leaf_axis)
    chol_id = lax.axis_index(chol_axis)

    lane = lax.broadcasted_iota(jnp.int32, (B, B), 1)
    sub = lax.broadcasted_iota(jnp.int32, (B, B), 0)

    row_form, col_form = [], []
    for k in range(nblk):
        if k < nc:
            blk = got_ref[:, k * B:(k + 1) * B]
            alive = (idx_ref[:, k * B:(k + 1) * B] // own != leaf_id).astype(f32)
            vals = blk[3:] * alive
            vals2 = vals
        else:
            blk = own_ref[:, (k - nc) * B:(k - nc + 1) * B]
            alive = jnp.ones((1, B), f32)
            vals = blk[3:]
            vals2 = jnp.zeros_like(vals)
        stack = jnp.concatenate(
            [vals, vals2, blk[:3], alive, jnp.zeros((B - 2 * cols - 4, B), f32)], axis=0)
        t = stack.T
        row_form.append((blk[0:1], blk[1:2], blk[2:3], alive))
        c0 = 2 * cols
        col_form.append(tuple(jnp.broadcast_to(t[:, c0 + i:c0 + i + 1], (B, B)) for i in range(4)))
        a_ref[k * B:(k + 1) * B, total:total + B] = jnp.where(lane < c0, t, 0.0)

    for k in range(nblk):
        cx, cy, cz, ca = col_form[k]
        for c in range(nblk):
            if c < k:
                a_ref[k * B:(k + 1) * B, c * B:(c + 1) * B] = jnp.zeros((B, B), f32)
                continue
            rx, ry, rz, ra = row_form[c]
            dx, dy, dz = cx - rx, cy - ry, cz - rz
            sq = jnp.maximum(dx * dx + dy * dy + dz * dz, 1e-30)
            dist = sq * lax.rsqrt(sq)
            kern = jnp.exp(dist * (-1.0 / length_scale)) * (ca * ra)
            if c == k:
                kern = jnp.where(lane == sub, kern + (nugget * ra + 1.0 - ra), kern)
            a_ref[k * B:(k + 1) * B, c * B:(c + 1) * B] = kern

    lane8 = lax.broadcasted_iota(jnp.int32, (8, B), 1)
    sub8 = lax.broadcasted_iota(jnp.int32, (8, B), 0)

    def spread(x, i):
        return jnp.broadcast_to(x[:, i:i + 1], (8, B))

    def chol8(S, rows):
        scales = []
        for j in range(8):
            r = lax.rsqrt(S[j][j])
            scales.append(r)
            rows[j] = rows[j] * r
            for i in range(j + 1, 8):
                S[i][j] = S[i][j] * r
            for i in range(j + 1, 8):
                for c in range(j + 1, i + 1):
                    S[i][c] = S[i][c] - S[i][j] * S[c][j]
            for i in range(j + 1, 8):
                rows[i] = rows[i] - S[i][j] * rows[j]
        return scales

    def block_step(k, carry):
        row0 = pl.multiple_of(k * B, B)
        d_ref[...] = a_ref[pl.ds(row0, B), pl.ds(row0, B)]
        for s in range(B // G):
            base = s * G
            pivot = (lane8 >= base) & (lane8 < base + G)
            p0 = d_ref[base:base + 8, :]
            p1 = d_ref[base + 8:base + 16, :]
            for c in range(8):
                v_ref[s % 2, 0, c] = spread(p0, base + c)
            V = [spread(p1, base + c) for c in range(16)]
            S = [[jnp.broadcast_to(v_ref[s % 2, 0, c, i:i + 1, :], (8, B)) for c in range(i + 1)] for i in range(8)]
            x0 = jnp.where(pivot, (lane8 == base + sub8).astype(f32), p0)
            x1 = jnp.where(pivot, (lane8 == base + 8 + sub8).astype(f32), p1)
            x_ref[s % 2, 0] = x0
            R = [jnp.broadcast_to(x_ref[s % 2, 0, i:i + 1, :], (8, B)) for i in range(8)]
            scales = chol8(S, R)
            for j in range(8):
                V[j] = V[j] * scales[j]
                for c in range(j + 1, 8):
                    V[c] = V[c] - V[j] * S[c][j]
                v_ref[s % 2, 1, j] = V[j]
                x1 = x1 - V[j] * R[j]
                for c in range(8):
                    V[8 + c] = V[8 + c] - V[j] * jnp.broadcast_to(v_ref[s % 2, 1, j, c:c + 1, :], (8, B))
            for c in range(8):
                v_ref[s % 2, 2, c] = V[8 + c]
            x_ref[s % 2, 1] = x1
            S1 = [[jnp.broadcast_to(v_ref[s % 2, 2, c, i:i + 1, :], (8, B)) for c in range(i + 1)] for i in range(8)]
            R1 = [jnp.broadcast_to(x_ref[s % 2, 1, i:i + 1, :], (8, B)) for i in range(8)]
            chol8(S1, R1)
            R = R + R1
            for i in range(G):
                w_ref[base + i:base + i + 1, :] = R[i][0:1, :]
            for g in range(2 * (s + 1), B // 8):
                index = sub8 + 8 * g
                acc = jnp.where(pivot, 0.0, d_ref[8 * g:8 * g + 8, :])
                for j in range(G):
                    acc = acc - jnp.take_along_axis(R[j], index, axis=1, mode="promise_in_bounds") * R[j]
                d_ref[8 * g:8 * g + 8, :] = acc
        w = jnp.where(lane <= sub, w_ref[...], 0.0)
        wh, wm = halves(w)
        wst = jnp.concatenate([wh, wh, wm], axis=1)
        for t in range(nblk):
            @pl.when(k == t)
            def _(t=t):
                at = a_ref[t * B:(t + 1) * B, (t + 1) * B:]
                ah, am = halves(at)
                panel = jnp.dot(wst, jnp.concatenate([ah, am, ah], axis=0), preferred_element_type=f32)
                z_ref[t * B:(t + 1) * B, :] = panel[:, -B:]
                if t + 1 == nblk:
                    return
                ph, pm = halves(panel)
                right = jnp.concatenate([ph, pm, ph], axis=0)
                left = jnp.concatenate([ph, ph, pm], axis=0)
                for j in range(t + 1, nblk):
                    lo = (j - t - 1) * B
                    upd = lax.dot_general(left[:, lo:lo + B], right[:, lo:], (((0,), (0,)), ((), ())),
                                          preferred_element_type=f32)
                    a_ref[j * B:(j + 1) * B, j * B:] = a_ref[j * B:(j + 1) * B, j * B:] - upd
                if t == nc - 1:
                    m_ref[...] = -a_ref[cond:, total:total + B]
        return carry

    lax.fori_loop(0, nblk, block_step, 0)
    out = mean_ref.shape[1]
    start = pl.multiple_of(chol_id * out, 8)
    pad = jnp.zeros((B - out, B), f32)
    mt = jnp.concatenate([m_ref[pl.ds(start, out), :], pad], axis=0).T
    zt = jnp.concatenate([z_ref[pl.ds(cond + start, out), :], pad], axis=0).T
    mean_ref[...] = mt[cols:2 * cols, :out]
    white_ref[...] = zt[:cols, :out]


def on_device(leaves, chols, coords, observed, cond_index):
    leaf_id = lax.axis_index("leaf")
    own = coords.shape[1]
    cond = cond_index.shape[1]
    cols = observed.shape[0]
    packed = jnp.concatenate([coords, observed], axis=0)
    every = lax.all_to_all(jnp.broadcast_to(packed[None], (leaves,) + packed.shape), "leaf", 0, 0)
    every = jnp.swapaxes(every, 0, 1).reshape(packed.shape[0], leaves * own)
    got = jnp.take(every, cond_index[0], axis=1)
    out = own // chols
    total = own + cond
    return pl.pallas_call(
        functools.partial(kernel, "leaf", "chol"),
        out_shape=(jax.ShapeDtypeStruct((cols, out), f32),) * 2,
        in_specs=[pl.BlockSpec(memory_space=pltpu.VMEM)] * 3,
        out_specs=(pl.BlockSpec(memory_space=pltpu.VMEM),) * 2,
        scratch_shapes=[
            pltpu.VMEM((total, total + B), f32),
            pltpu.VMEM((B, B), f32),
            pltpu.VMEM((2, 3, 8, 8, B), f32),
            pltpu.VMEM((2, 2, 8, B), f32),
            pltpu.VMEM((B, B), f32),
            pltpu.VMEM((total, B), f32),
            pltpu.VMEM((own, B), f32),
        ],
        compiler_params=pltpu.CompilerParams(vmem_limit_bytes=48 << 20),
        name="vecchia",
    )(got, packed, cond_index)


def solution(mesh):
    return jax.shard_map(
        functools.partial(on_device, mesh.shape["leaf"], mesh.shape["chol"]),
        mesh=mesh,
        in_specs=(P(None, "leaf"), P(None, "leaf"), P("leaf", None)),
        out_specs=(P(None, ("leaf", "chol")), P(None, ("leaf", "chol"))),
        check_vma=False,
    )
```

time: 84.7 us -> 48.3 us (0.57)
  blocking collectives: 32.6 us -> 0 us
  Pallas kernels: 48.7 us -> 27.1 us
  waiting for transfers between devices: 0 us -> 8.23 us
  starting transfers between devices: 0 us -> 7.44 us
  other arithmetic: 0.78 us -> 2.14 us
    all_gather x1 -> x0, blocking collectives: 32.6 us -> none  [on_device(): every = lax.all_gather(packed, 'leaf', axis=1, tiled=True)]
    pallas_call x1, Pallas kernels: 48.7 us -> 27.1 us  [on_device(): pl.pallas_call(functools.partial(kernel, 'leaf', 'chol'), out_shape=(jax....]
    all_to_all x0 -> x1, waiting for transfers between devices: none -> 8.23 us  [on_device(): lax.all_to_all(jnp.broadcast_to(packed[None], (leaves,) + packed.shape),...]
    all_to_all x0 -> x1, starting transfers between devices: none -> 7.44 us  [on_device(): lax.all_to_all(jnp.broadcast_to(packed[None], (leaves,) + packed.shape),...]
  transfers between devices with their start and end apart: 0 -> 1, of which waited for: 0 -> 1; matrix products, arithmetic and copies ran while one was open for 0% -> 3% of each run, Pallas kernels for 0% -> 0%
where the time goes in v1:
time: 48.3 us; the launch traced here: 48 us
  Pallas kernels  27.1 us (56%)
  waiting for transfers between devices  8.23 us (17%)
  starting transfers between devices  7.44 us (15%)
  local copies, waits for them, and re-layouts  2.37 us (5%)
  other arithmetic  2.14 us (4%)
  between operations  0.67 us (1%)
    pallas_call x1, Pallas kernels, on_device(): pl.pallas_call(functools.partial(kernel, 'leaf', 'chol'), out_shape=(jax....  27.1 us
    all_to_all x1, waiting for transfers between devices, on_device(): lax.all_to_all(jnp.broadcast_to(packed[None], (leaves,) + packed.shape),...  8.23 us
    all_to_all x1, starting transfers between devices, on_device(): lax.all_to_all(jnp.broadcast_to(packed[None], (leaves,) + packed.shape),...  7.44 us
    gather x2, local copies, waits for them, and re-layouts, on_device(): got = jnp.take(every, cond_index[0], axis=1)  1.15 us
  transfers between devices with their start and end apart: 1, of which 1 were waited for; matrix products, arithmetic and copies ran while one was open for 3% of the time, Pallas kernels for 0%

profile of v1, /device:TPU:0, one launch (start us, length us, event | category | flops | bytes accessed | tf_op | source)
XLA Modules:
  0.0 48.0 jit_solution(1115141994567563890)
XLA Ops:
  0.6 0.7 %pad_maximum_fusion.own_ref = f32[19,384]{1,0:T(8,128)S(1)} fusion(f32[16,384]{1,0:T(8,128)} %param.4, f32[3,384]{1,0:T(4,128)} %param.3), kind=kLoop, calls=%fused_computation.2 | loop fusion | flops 7296 | bytes 58368 | tf_op jit(solution)/shard_map/concatenate | solution.py:172
  1.4 0.7 %broadcast_in_dim.17 = f32[8,19,384]{2,1,0:T(8,128)} broadcast(f32[19,384]{1,0:T(8,128)S(1)} %pad_maximum_fusion.own_ref), dimensions={1,2} | broadcast | bytes 262656 | tf_op jit(solution)/shard_map/broadcast_in_dim | solution.py:173
  2.1 0.0 copy-start
  2.1 7.4 %all-to-all-start = ((f32[8,19,384]{2,1,0:T(8,128)}), f32[8,19,384]{2,1,0:T(8,128)S(1)}, u32[]{:S(2)}, u32[]{:S(2)}) async-start(f32[8,19,384]{2,1,0:T(8,128)} %broadcast_in_dim.17), calls=%async_computation | async-start | bytes 589824 | tf_op jit(solution)/shard_map/all_to_all | solution.py:173
  9.5 0.7 %compare_select_fusion = s32[512,1]{0,1:T(1,128)S(1)} fusion(s32[1,512]{1,0:T(1,128)} %idx_ref.1), kind=kLoop, calls=%fused_computation.3 | loop fusion | flops 1536 | bytes 4096 | tf_op jit(solution)/shard_map/jit(_take)/jit(_where)/select_n | solution.py:175
  10.2 0.7 %compare_and_fusion = pred[512]{0:T(512)(128)(4,1)S(1)} fusion(s32[512]{0:T(512)} %bitcast.8), kind=kLoop, calls=%fused_computation.6 | loop fusion | flops 3072 | bytes 2560 | tf_op jit(solution)/shard_map/jit(_take)/and | solution.py:175
  10.9 8.2 %all-to-all-done = f32[8,19,384]{2,1,0:T(8,128)S(1)} async-done(((f32[8,19,384]{2,1,0:T(8,128)}), f32[8,19,384]{2,1,0:T(8,128)S(1)}, u32[]{:S(2)}, u32[]{:S(2)}) %all-to-all-start) | async-done | bytes 233504 | tf_op jit(solution)/shard_map/all_to_all | solution.py:173
  19.2 0.5 %copy.9 = f32[19,8,384]{0,2,1:T(8,128)S(1)} copy(f32[19,8,384]{2,0,1:T(8,128)S(1)} %bitcast.10) | data formatting | bytes 466944 | tf_op jit(solution)/shard_map/transpose | solution.py:174
  19.7 1.0 %gather_fusion = f32[512,19]{1,0:T(8,128)S(1)} fusion(f32[19,3072]{0,1:T(8,128)S(1)} %bitcast.9, s32[1024]{0:T(1024)S(1)} %pad_clamp_fusion), kind=kCustom, calls=%fused_computation | custom fusion | bytes 79872 | tf_op jit(solution)/shard_map/jit(_take)/gather | solution.py:175
  20.7 0.1 copy.10
  20.8 0.0 copy-done
  20.8 27.1 %vecchia.1 = (f32[16,96]{1,0:T(8,128)}, f32[16,96]{1,0:T(8,128)}) custom-call(f32[19,512]{1,0:T(8,128)S(1)} %select_bitcast_fusion.got_ref, f32[19,384]{1,0:T(8,128)S(1)} %pad_maximum_fusion.own_ref, s32[1,512]{1,0:T(1,128)S(1)} %copy-done), custom_call_target="tpu_custom_call" | custom-call | tf_op jit(solution)/shard_map/vecchia/pallas_call | solution.py:178
  (2 shorter events, 0.0 us)
Async XLA Ops:
  2.1 18.7 %copy-start = (s32[1,512]{1,0:T(1,128)S(1)}, s32[1,512]{1,0:T(1,128)}, u32[]{:S(2)}) copy-start(s32[1,512]{1,0:T(1,128)} %idx_ref.1) | copy-start | bytes 6148
  2.1 17.1 %all-to-all-start = ((f32[8,19,384]{2,1,0:T(8,128)}), f32[8,19,384]{2,1,0:T(8,128)S(1)}, u32[]{:S(2)}, u32[]{:S(2)}) async-start(f32[8,19,384]{2,1,0:T(8,128)} %broadcast_in_dim.17), calls=%async_computation | async-start | bytes 589824 | tf_op jit(solution)/shard_map/all_to_all | solution.py:173

commit v2 on v1

--- a/solution.py
+++ b/solution.py
@@ -20,10 +20,21 @@
     return high, (x - high.astype(f32)).astype(bf16)
 
 
-def kernel(leaf_axis, chol_axis, got_ref, own_ref, idx_ref, mean_ref, white_ref,
-           a_ref, d_ref, v_ref, x_ref, w_ref, z_ref, m_ref):
+def thirds(x):
+    high = x.astype(bf16)
+    rest = x - high.astype(f32)
+    mid = rest.astype(bf16)
+    return jnp.concatenate([high, mid, (rest - mid.astype(f32)).astype(bf16)], axis=0)
+
+
+def kernel(leaf_axis, chol_axis, masks, pos_ref, idx_ref, *refs):
+    npieces = len(refs) - 10
+    piece_refs = refs[:npieces]
+    (mean_ref, white_ref, a_ref, d_ref, v_ref, x_ref, w_ref, z_ref, m_ref,
+     g_ref) = refs[npieces:]
+    own_ref = piece_refs[0]
     own = own_ref.shape[1]
-    cond = got_ref.shape[1]
+    cond = idx_ref.shape[1]
     cols = own_ref.shape[0] - 3
     total = cond + own
     nblk = total // B
@@ -35,9 +46,30 @@
     sub = lax.broadcasted_iota(jnp.int32, (B, B), 0)
 
     row_form, col_form = [], []
+    if masks:
+        i = 0
+        for piece in piece_refs:
+            tail = g_ref.shape[1] - piece.shape[0]
+            for lo in range(0, piece.shape[1], own):
+                g_ref[i] = jnp.concatenate([piece[:, lo:lo + own], jnp.zeros((tail, own), f32)], axis=0)
+                i += 1
     for k in range(nblk):
         if k < nc:
-            blk = got_ref[:, k * B:(k + 1) * B]
+            if masks:
+                far = pos_ref[0, k * B] // own ^ leaf_id
+                place = 0
+                for i, mask in enumerate(masks):
+                    if i:
+                        here = jnp.where(chol_id % 2 == 0, mask % 256, mask // 256)
+                        place = jnp.where((far == here) & (here > 0), i, place)
+                site = idx_ref[:, k * B:(k + 1) * B] % own
+                hot = (lax.broadcasted_iota(jnp.int32, (own, B), 0) == site).astype(f32).astype(bf16)
+                parts = jnp.dot(thirds(g_ref[place]), hot, preferred_element_type=f32)
+                third = parts.shape[0] // 3
+                blk = parts[:third] + parts[third:2 * third] + parts[2 * third:]
+                blk = blk[:cols + 3]
+            else:
+                blk = piece_refs[1][:, k * B:(k + 1) * B]
             alive = (idx_ref[:, k * B:(k + 1) * B] // own != leaf_id).astype(f32)
             vals = blk[3:] * alive
             vals2 = vals
@@ -165,20 +197,45 @@
 
 
 def on_device(leaves, chols, coords, observed, cond_index):
-    leaf_id = lax.axis_index("leaf")
     own = coords.shape[1]
     cond = cond_index.shape[1]
     cols = observed.shape[0]
     packed = jnp.concatenate([coords, observed], axis=0)
-    every = lax.all_to_all(jnp.broadcast_to(packed[None], (leaves,) + packed.shape), "leaf", 0, 0)
-    every = jnp.swapaxes(every, 0, 1).reshape(packed.shape[0], leaves * own)
-    got = jnp.take(every, cond_index[0], axis=1)
     out = own // chols
     total = own + cond
+    bits = leaves.bit_length() - 1
+    masks = tuple((1 << t) ^ (1 << (t - 1) if t > 1 else 0) for t in range(bits))
+    grouped = 2 * cond // leaves % B == 0
+    labels = [0]
+    if grouped:
+        pieces = [packed]
+        def swap(even, odd):
+            return [(j * chols + c, (j ^ (odd if c % 2 else even)) * chols + c)
+                    for j in range(leaves) for c in range(chols) if (odd if c % 2 else even)]
+        plan = [(m + (m >> 1 & 1), m + 1 - (m >> 1 & 1)) for m in range(0, leaves, 2)]
+        got = [lax.ppermute(packed, ("leaf", "chol"), swap(*p)) for p in plan]
+        cross = [(j, j ^ 1) for j in range(chols)]
+        pieces += got + [lax.ppermute(g, "chol", cross) for g in got]
+        labels = [0] + [p[0] + 256 * p[1] for p in plan] + [p[1] + 256 * p[0] for p in plan]
+        rows = -(-packed.shape[0] // 8) * 8
+    else:
+        every = packed
+        for mask in masks:
+            swap = [(j, j ^ mask) for j in range(leaves)]
+            every = jnp.concatenate([every, lax.ppermute(every, "leaf", swap)], axis=1)
+        far = cond_index[0] // own ^ lax.axis_index("leaf")
+        place = jnp.zeros_like(far)
+        for bit in range(bits - 1, -1, -1):
+            has = (far >> bit) & 1
+            place = place + (has << bit)
+            far = far ^ (has * masks[bit])
+        pieces = [packed, jnp.take(every, place * own + cond_index[0] % own, axis=1)]
+        rows = 8
     return pl.pallas_call(
-        functools.partial(kernel, "leaf", "chol"),
+        functools.partial(kernel, "leaf", "chol", tuple(labels) if grouped else ()),
         out_shape=(jax.ShapeDtypeStruct((cols, out), f32),) * 2,
-        in_specs=[pl.BlockSpec(memory_space=pltpu.VMEM)] * 3,
+        in_specs=[pl.BlockSpec(memory_space=pltpu.SMEM)]
+        + [pl.BlockSpec(memory_space=pltpu.VMEM)] * (1 + len(pieces)),
         out_specs=(pl.BlockSpec(memory_space=pltpu.VMEM),) * 2,
         scratch_shapes=[
             pltpu.VMEM((total, total + B), f32),
@@ -188,10 +245,11 @@
             pltpu.VMEM((B, B), f32),
             pltpu.VMEM((total, B), f32),
             pltpu.VMEM((own, B), f32),
+            pltpu.VMEM((leaves + 1 if grouped else 1, rows, own), f32),
         ],
         compiler_params=pltpu.CompilerParams(vmem_limit_bytes=48 << 20),
         name="vecchia",
-    )(got, packed, cond_index)
+    )(cond_index, cond_index, *pieces)
 
 
 def solution(mesh):

time: 48.3 us -> 42.1 us (0.87)
  waiting for transfers between devices: 8.23 us -> 4.59 us
  local copies, waits for them, and re-layouts: 2.37 us -> 0.01 us
  other arithmetic: 2.14 us -> 0.75 us
  Pallas kernels: 27.1 us -> 27.9 us
  starting transfers between devices: 7.44 us -> 8.02 us
    all_to_all x1 -> x0, waiting for transfers between devices: 8.23 us -> none  [on_device(): lax.all_to_all(jnp.broadcast_to(packed[None], (leaves,) + packed.shape),...]
    ppermute x0 -> x8, starting transfers between devices: none -> 8.02 us  [the longest x4 7.32 us: on_device(): got = [lax.ppermute(packed, ('leaf', 'chol'), swap(*p)) for p in plan]]
    all_to_all x1 -> x0, starting transfers between devices: 7.44 us -> none  [on_device(): lax.all_to_all(jnp.broadcast_to(packed[None], (leaves,) + packed.shape),...]
    ppermute x0 -> x8, waiting for transfers between devices: none -> 4.59 us  [the longest x4 3.71 us: on_device(): got = [lax.ppermute(packed, ('leaf', 'chol'), swap(*p)) for p in plan]]
    gather x2 -> x0, local copies, waits for them, and re-layouts: 1.15 us -> none  [on_device(): got = jnp.take(every, cond_index[0], axis=1)]
    pallas_call x1, Pallas kernels: 27.1 us -> 27.9 us  [on_device(): pl.pallas_call(functools.partial(kernel, 'leaf', 'chol', tuple(labels) if...]
    broadcast_in_dim x1 -> x0, local copies, waits for them, and re-layouts: 0.72 us -> none  [on_device(): jnp.broadcast_to(packed[None], (leaves,) + packed.shape)]
    select_n x2 -> x0, other arithmetic: 0.69 us -> none  [on_device(): got = jnp.take(every, cond_index[0], axis=1)]
  transfers between devices with their start and end apart: 1 -> 8, of which waited for: 1 -> 6; matrix products, arithmetic and copies ran while one was open for 3% -> 0% of each run, Pallas kernels for 0% -> 0%
where the time goes in v2:
time: 42.1 us; the launch traced here: 42 us
  Pallas kernels  27.9 us (66%)
  starting transfers between devices  8.02 us (19%)
  waiting for transfers between devices  4.59 us (11%)
  other arithmetic  0.75 us (2%)
  between operations  0.65 us (2%)
    pallas_call x1, Pallas kernels, on_device(): pl.pallas_call(functools.partial(kernel, 'leaf', 'chol', tuple(labels) if...  27.9 us
    ppermute x4, starting transfers between devices, on_device(): got = [lax.ppermute(packed, ('leaf', 'chol'), swap(*p)) for p in plan]  7.32 us
    ppermute x4, waiting for transfers between devices, on_device(): got = [lax.ppermute(packed, ('leaf', 'chol'), swap(*p)) for p in plan]  3.71 us
    ppermute x4, waiting for transfers between devices, on_device(): pieces += got + [lax.ppermute(g, 'chol', cross) for g in got]  0.88 us
  transfers between devices with their start and end apart: 8, of which 6 were waited for; matrix products, arithmetic and copies ran while one was open for 0% of the time, Pallas kernels for 0%

profile of v2, /device:TPU:0, one launch (start us, length us, event | category | flops | bytes accessed | tf_op | source)
XLA Modules:
  0.0 42.0 jit_solution(6583481164827907558)
XLA Ops:
  0.6 0.0 copy-start
  0.6 0.8 %pad_maximum_fusion.refs_0_ = f32[19,384]{1,0:T(8,128)S(1)} fusion(f32[16,384]{1,0:T(8,128)} %param.4, f32[3,384]{1,0:T(4,128)} %param.3), kind=kLoop, calls=%fused_computation | loop fusion | flops 7296 | bytes 58368 | tf_op jit(solution)/shard_map/concatenate | solution.py:203
  1.4 6.0 %collective-permute-start.3 = (f32[19,384]{1,0:T(8,128)S(1)}, f32[19,384]{1,0:T(8,128)S(1)}, u32[]{:S(2)}, u32[]{:S(2)}) collective-permute-start(f32[19,384]{1,0:T(8,128)S(1)} %pad_maximum_fusion.refs_0_), channel_id=1, source_target_pairs={{0,28},{1,25},{2,30},{3,27},{4,24},{5,29},{6,26},{7,31},{8,20},{9,... | collective-permute-start | bytes 87560 | tf_op jit(solution)/shard_map/ppermute | solution.py:216
  7.4 0.0 collective-permute-start.2
  7.4 0.6 %collective-permute-start.1 = (f32[19,384]{1,0:T(8,128)S(1)}, f32[19,384]{1,0:T(8,128)S(1)}, u32[]{:S(2)}, u32[]{:S(2)}) collective-permute-start(f32[19,384]{1,0:T(8,128)S(1)} %pad_maximum_fusion.refs_0_), channel_id=1, source_target_pairs={{0,12},{1,9},{2,14},{3,11},{4,8},{5,13},{6,10},{7,15},{8,4},{9,1},... | collective-permute-start | bytes 87560 | tf_op jit(solution)/shard_map/ppermute | solution.py:216
  8.1 0.7 %collective-permute-start = (f32[19,384]{1,0:T(8,128)S(1)}, f32[19,384]{1,0:T(8,128)S(1)}, u32[]{:S(2)}, u32[]{:S(2)}) collective-permute-start(f32[19,384]{1,0:T(8,128)S(1)} %pad_maximum_fusion.refs_0_), channel_id=1, source_target_pairs={{1,5},{3,7},{5,1},{7,3},{9,13},{11,15},{13,9},{15,11},{17,21},{19,... | collective-permute-start | bytes 87560 | tf_op jit(solution)/shard_map/ppermute | solution.py:216
  8.7 0.6 %collective-permute-done.3.refs_4_ = f32[19,384]{1,0:T(8,128)S(1)} collective-permute-done((f32[19,384]{1,0:T(8,128)S(1)}, f32[19,384]{1,0:T(8,128)S(1)}, u32[]{:S(2)}, u32[]{:S(2)}) %collective-permute-start.3) | collective-permute-done | bytes 29216 | tf_op jit(solution)/shard_map/ppermute | solution.py:216
  9.4 0.2 collective-permute-start.7
  9.5 2.7 %collective-permute-done.2.refs_3_ = f32[19,384]{1,0:T(8,128)S(1)} collective-permute-done((f32[19,384]{1,0:T(8,128)S(1)}, f32[19,384]{1,0:T(8,128)S(1)}, u32[]{:S(2)}, u32[]{:S(2)}) %collective-permute-start.2) | collective-permute-done | bytes 29216 | tf_op jit(solution)/shard_map/ppermute | solution.py:216
  12.3 0.0 collective-permute-start.6
  12.3 0.3 collective-permute-done.1.refs_2_
  12.6 0.2 collective-permute-start.5
  12.8 0.0 collective-permute-done.refs_1_
  12.8 0.3 collective-permute-start.4
  13.1 0.0 collective-permute-done.7.refs_8_
  13.1 0.4 collective-permute-done.6.refs_7_
  13.5 0.3 collective-permute-done.5.refs_6_
  13.8 0.2 collective-permute-done.4.refs_5_
  14.0 0.0 copy-done
  14.0 27.9 %vecchia.1 = (f32[16,96]{1,0:T(8,128)}, f32[16,96]{1,0:T(8,128)}) custom-call(s32[1,512]{1,0:T(1,128)S(1)} %copy-done, s32[1,512]{1,0:T(1,128)S(1)} %copy-done, f32[19,384]{1,0:T(8,128)S(1)} %pad_maximum_fusion.refs_0_, f32[19,384]{1,0:T(8,128)S(1)} %collective-permute-done.refs_1_, f32[19,384]{1,0:T(8,128)S(1)} %collective-permute-done.1.refs_2_, ...), custom_call_target="tpu_custom_call" | custom-call | tf_op jit(solution)/shard_map/vecchia/pallas_call | solution.py:234
Async XLA Ops:
  0.6 13.4 %copy-start = (s32[1,512]{1,0:T(1,128)S(1)}, s32[1,512]{1,0:T(1,128)}, u32[]{:S(2)}) copy-start(s32[1,512]{1,0:T(1,128)} %idx_ref.1) | copy-start | bytes 6148
  1.4 8.0 %collective-permute-start.3 = (f32[19,384]{1,0:T(8,128)S(1)}, f32[19,384]{1,0:T(8,128)S(1)}, u32[]{:S(2)}, u32[]{:S(2)}) collective-permute-start(f32[19,384]{1,0:T(8,128)S(1)} %pad_maximum_fusion.refs_0_), channel_id=1, source_target_pairs={{0,28},{1,25},{2,30},{3,27},{4,24},{5,29},{6,26},{7,31},{8,20},{9,... | collective-permute-start | bytes 87560 | tf_op jit(solution)/shard_map/ppermute | solution.py:216
  7.4 4.9 %collective-permute-start.2 = (f32[19,384]{1,0:T(8,128)S(1)}, f32[19,384]{1,0:T(8,128)S(1)}, u32[]{:S(2)}, u32[]{:S(2)}) collective-permute-start(f32[19,384]{1,0:T(8,128)S(1)} %pad_maximum_fusion.refs_0_), channel_id=1, source_target_pairs={{0,16},{1,21},{2,18},{3,23},{4,20},{5,17},{6,22},{7,19},{8,24},{9,... | collective-permute-start | bytes 87560 | tf_op jit(solution)/shard_map/ppermute | solution.py:216
  7.4 5.2 %collective-permute-start.1 = (f32[19,384]{1,0:T(8,128)S(1)}, f32[19,384]{1,0:T(8,128)S(1)}, u32[]{:S(2)}, u32[]{:S(2)}) collective-permute-start(f32[19,384]{1,0:T(8,128)S(1)} %pad_maximum_fusion.refs_0_), channel_id=1, source_target_pairs={{0,12},{1,9},{2,14},{3,11},{4,8},{5,13},{6,10},{7,15},{8,4},{9,1},... | collective-permute-start | bytes 87560 | tf_op jit(solution)/shard_map/ppermute | solution.py:216
  8.1 4.7 %collective-permute-start = (f32[19,384]{1,0:T(8,128)S(1)}, f32[19,384]{1,0:T(8,128)S(1)}, u32[]{:S(2)}, u32[]{:S(2)}) collective-permute-start(f32[19,384]{1,0:T(8,128)S(1)} %pad_maximum_fusion.refs_0_), channel_id=1, source_target_pairs={{1,5},{3,7},{5,1},{7,3},{9,13},{11,15},{13,9},{15,11},{17,21},{19,... | collective-permute-start | bytes 87560 | tf_op jit(solution)/shard_map/ppermute | solution.py:216
  9.4 3.8 %collective-permute-start.7 = (f32[19,384]{1,0:T(8,128)S(1)}, f32[19,384]{1,0:T(8,128)S(1)}, u32[]{:S(2)}, u32[]{:S(2)}) collective-permute-start(f32[19,384]{1,0:T(8,128)S(1)} %collective-permute-done.3.refs_4_), channel_id=1, source_target_pairs={{0,1},{1,0},{2,3},{3,2},{4,5},{5,4},{6,7},{7,6},{8,9},{9,8},{10,11... | collective-permute-start | bytes 87560 | tf_op jit(solution)/shard_map/ppermute | solution.py:218
  12.3 1.2 %collective-permute-start.6 = (f32[19,384]{1,0:T(8,128)S(1)}, f32[19,384]{1,0:T(8,128)S(1)}, u32[]{:S(2)}, u32[]{:S(2)}) collective-permute-start(f32[19,384]{1,0:T(8,128)S(1)} %collective-permute-done.2.refs_3_), channel_id=1, source_target_pairs={{0,1},{1,0},{2,3},{3,2},{4,5},{5,4},{6,7},{7,6},{8,9},{9,8},{10,11... | collective-permute-start | bytes 87560 | tf_op jit(solution)/shard_map/ppermute | solution.py:218
  12.6 1.2 %collective-permute-start.5 = (f32[19,384]{1,0:T(8,128)S(1)}, f32[19,384]{1,0:T(8,128)S(1)}, u32[]{:S(2)}, u32[]{:S(2)}) collective-permute-start(f32[19,384]{1,0:T(8,128)S(1)} %collective-permute-done.1.refs_2_), channel_id=1, source_target_pairs={{0,1},{1,0},{2,3},{3,2},{4,5},{5,4},{6,7},{7,6},{8,9},{9,8},{10,11... | collective-permute-start | bytes 87560 | tf_op jit(solution)/shard_map/ppermute | solution.py:218
  12.8 1.2 %collective-permute-start.4 = (f32[19,384]{1,0:T(8,128)S(1)}, f32[19,384]{1,0:T(8,128)S(1)}, u32[]{:S(2)}, u32[]{:S(2)}) collective-permute-start(f32[19,384]{1,0:T(8,128)S(1)} %collective-permute-done.refs_1_), channel_id=1, source_target_pairs={{0,1},{1,0},{2,3},{3,2},{4,5},{5,4},{6,7},{7,6},{8,9},{9,8},{10,11... | collective-permute-start | bytes 87560 | tf_op jit(solution)/shard_map/ppermute | solution.py:218

commit v3 on v2

v3 whole, which is shorter than its diff:
```python
import functools
import jax
import jax.numpy as jnp
from jax import lax
from jax.experimental import pallas as pl
from jax.experimental.pallas import tpu as pltpu
from jax.sharding import PartitionSpec as P

length_scale = 0.3
nugget = 0.2
B = 128
G = 16
LANES = 128
f32 = jnp.float32
bf16 = jnp.bfloat16


def thirds(x):
    high = x.astype(bf16)
    rest = x - high.astype(f32)
    mid = rest.astype(bf16)
    return high, mid, (rest - mid.astype(f32)).astype(bf16)


def kernel(leaf_axis, chol_axis, masks, pos_ref, idx_ref, *refs):
    npieces = len(refs) - 15
    piece_refs = refs[:npieces]
    (mean_ref, white_ref, a_ref, d_ref, v_ref, x_ref, w_ref, z_ref, m_ref,
     g_ref, f_ref, w3_ref, p3_ref, pt_ref, n_ref) = refs[npieces:]
    own_ref = piece_refs[0]
    own = own_ref.shape[1]
    cond = idx_ref.shape[1]
    cols = own_ref.shape[0] - 3
    total = cond + own
    nblk = total // B
    nc = cond // B
    leaf_id = lax.axis_index(leaf_axis)
    chol_id = lax.axis_index(chol_axis)

    lane = lax.broadcasted_iota(jnp.int32, (B, B), 1)
    sub = lax.broadcasted_iota(jnp.int32, (B, B), 0)

    if masks:
        i = 0
        for piece in piece_refs:
            tail = g_ref.shape[1] - piece.shape[0]
            for lo in range(0, piece.shape[1], own):
                g_ref[i] = jnp.concatenate([piece[:, lo:lo + own], jnp.zeros((tail, own), f32)], axis=0)
                i += 1
    row_form = []
    c0 = 2 * cols
    for k in range(nblk):
        if k < nc:
            if masks:
                far = pos_ref[0, k * B] // own ^ leaf_id
                place = 0
                for i, mask in enumerate(masks):
                    if i:
                        here = jnp.where(chol_id % 2 == 0, mask % 256, mask // 256)
                        place = jnp.where((far == here) & (here > 0), i, place)
                site = idx_ref[:, k * B:(k + 1) * B] % own
                hot = (lax.broadcasted_iota(jnp.int32, (own, B), 0) == site).astype(f32).astype(bf16)
                parts = jnp.dot(jnp.concatenate(thirds(g_ref[place]), axis=0), hot, preferred_element_type=f32)
                third = parts.shape[0] // 3
                blk = parts[:third] + parts[third:2 * third] + parts[2 * third:]
                blk = blk[:cols + 3]
            else:
                blk = piece_refs[1][:, k * B:(k + 1) * B]
            alive = (idx_ref[:, k * B:(k + 1) * B] // own != leaf_id).astype(f32)
            vals = blk[3:] * alive
            vals2 = vals
        else:
            blk = own_ref[:, (k - nc) * B:(k - nc + 1) * B]
            alive = jnp.ones((1, B), f32)
            vals = blk[3:]
            vals2 = jnp.zeros_like(vals)
        stack = jnp.concatenate(
            [vals, vals2, blk[:3], alive, jnp.zeros((B - c0 - 4, B), f32)], axis=0)
        t = stack.T
        f_ref[:, k * B:(k + 1) * B] = jnp.concatenate([blk[:3], alive, jnp.zeros((4, B), f32)], axis=0)
        a_ref[k * B:(k + 1) * B, total:] = t

    def build(k, tiles):
        t = a_ref[k * B:(k + 1) * B, total:]
        cx, cy, cz, ca = (jnp.broadcast_to(t[:, c0 + i:c0 + i + 1], (B, B)) for i in range(4))
        for c in tiles:
            rx, ry, rz, ra = (f_ref[i:i + 1, c * B:(c + 1) * B] for i in range(4))
            dx, dy, dz = cx - rx, cy - ry, cz - rz
            sq = jnp.maximum(dx * dx + dy * dy + dz * dz, 1e-30)
            dist = sq * lax.rsqrt(sq)
            kern = jnp.exp(dist * (-1.0 / length_scale)) * (ca * ra)
            if c == k:
                kern = jnp.where(lane == sub, kern + (nugget * ra + 1.0 - ra), kern)
            a_ref[k * B:(k + 1) * B, c * B:(c + 1) * B] = kern

    lane8 = lax.broadcasted_iota(jnp.int32, (8, B), 1)
    sub8 = lax.broadcasted_iota(jnp.int32, (8, B), 0)
    steps = B // G

    def spread(x, i):
        return jnp.broadcast_to(x[:, i:i + 1], (8, B))

    def row(ref, i):
        return jnp.broadcast_to(ref[i:i + 1, :], (8, B))

    def chol8(S, rows):
        scales = []
        for j in range(0, 8, 2):
            d, low, e = S[j][j], S[j + 1][j], S[j + 1][j + 1]
            det = d * e - low * low
            r = lax.rsqrt(d)
            rd = lax.rsqrt(det)
            q = rd * r
            r1 = q * d
            for i in range(j + 2, 8):
                S[i][j + 1] = (S[i][j + 1] * d - low * S[i][j]) * q
                S[i][j] = S[i][j] * r
            S[j + 1][j] = low * r
            for i in range(j + 2, 8):
                for c in range(j + 2, i + 1):
                    S[i][c] = (S[i][c] - S[i][j] * S[c][j]) - S[i][j + 1] * S[c][j + 1]
            scales += [r, r1]
            rows[j] = rows[j] * r
            rows[j + 1] = (rows[j + 1] - S[j + 1][j] * rows[j]) * r1
            for i in range(j + 2, 8):
                rows[i] = (rows[i] - S[i][j] * rows[j]) - S[i][j + 1] * rows[j + 1]
        return scales
    def pivot_of(s):
        return (lane8 >= s * G) & (lane8 < s * G + G)

    def eliminate(s, R, groups):
        for g in groups:
            index = sub8 + 8 * g
            acc = jnp.where(pivot_of(s), 0.0, d_ref[8 * g:8 * g + 8, :])
            for j in range(G):
                acc = acc - gather(R[j], index) * R[j]
            d_ref[8 * g:8 * g + 8, :] = acc

    def gather(x, index):
        return jnp.take_along_axis(x, index, axis=1, mode="promise_in_bounds")
    def begin(par, p0, p1, base):
        for c in range(8): v_ref[par, 0, c] = spread(p0, base + c)
        for c in range(16): v_ref[par, 3 + c // 8, c % 8] = spread(p1, base + c)
    def chain(s):
        base = s * G; par = s % 2; nxt = 1 - par; pivot = pivot_of(s)
        S = [[row(v_ref.at[par, 0, c], i) for c in range(i + 1)] for i in range(8)]
        V = [v_ref[par, 3 + c // 8, c % 8] for c in range(16)]
        x0 = jnp.where(pivot, (lane8 == base + sub8).astype(f32), d_ref[base:base + 8, :])
        x1 = jnp.where(pivot, (lane8 == base + 8 + sub8).astype(f32), d_ref[base + 8:base + 16, :])
        x_ref[par, 0] = x0
        R = [row(x_ref.at[par, 0], i) for i in range(8)]
        scales = chol8(S, R)
        for j in range(8):
            V[j] = V[j] * scales[j]
            for c in range(j + 1, 8): V[c] = V[c] - V[j] * S[c][j]
            v_ref[par, 1, j] = V[j]
            x1 = x1 - V[j] * R[j]
            for c in range(8): V[8 + c] = V[8 + c] - V[j] * row(v_ref.at[par, 1, j], c)
        for c in range(8): v_ref[par, 2, c] = V[8 + c]
        x_ref[par, 1] = x1
        S1 = [[row(v_ref.at[par, 2, c], i) for c in range(i + 1)] for i in range(8)]
        R1 = [row(x_ref.at[par, 1], i) for i in range(8)]
        more = s + 1 < steps
        if more:
            nb = base + G
            i0, i1 = sub8 + nb, sub8 + nb + 8
            q0 = jnp.where(pivot, 0.0, d_ref[nb:nb + 8, :]); q1 = jnp.where(pivot, 0.0, d_ref[nb + 8:nb + 16, :])
            for j in range(8):
                q0 = q0 - gather(R[j], i0) * R[j]
                q1 = q1 - gather(R[j], i1) * R[j]
            N0 = [spread(q0, nb + c) for c in range(8)]
            N1 = [spread(q1, nb + c) for c in range(16)]
        chol8(S1, R1)
        for i in range(8):
            w_ref[base + i:base + i + 1, :] = R[i][0:1, :]
            w_ref[base + 8 + i:base + 9 + i, :] = R1[i][0:1, :]
        if more:
            for j in range(8):
                m0, m1 = gather(R1[j], i0), gather(R1[j], i1)
                q0 = q0 - m0 * R1[j]
                q1 = q1 - m1 * R1[j]
                n_ref[j, 0] = m0
                n_ref[j, 1] = m1
                for c in range(8):
                    e0, e1 = row(n_ref.at[j, 0], c), row(n_ref.at[j, 1], c)
                    N0[c] = N0[c] - m0 * e0
                    N1[c] = N1[c] - m1 * e0
                    N1[8 + c] = N1[8 + c] - m1 * e1
            d_ref[nb:nb + 8, :] = q0
            d_ref[nb + 8:nb + 16, :] = q1
            for c in range(8): v_ref[nxt, 0, c] = N0[c]
            for c in range(16): v_ref[nxt, 3 + c // 8, c % 8] = N1[c]
    def near2(s):
        R = [row(w_ref, s * G + i) for i in range(G)]
        eliminate(s, R, (2 * s + 4, 2 * s + 5))
    def distant(s):
        lo = (s + 3) * G
        if lo >= B: return
        parts = thirds(w_ref[s * G:s * G + G, :])
        left = jnp.concatenate([parts[i] for i in (0, 0, 1, 1, 0, 2)], axis=0)
        right = jnp.concatenate([parts[i] for i in (0, 1, 0, 1, 2, 0)], axis=0)
        upd = lax.dot_general(left, right, (((0,), (0,)), ((), ())), preferred_element_type=f32)
        keep = (lane8[:1] < s * G) | (lane8[:1] >= s * G + G)
        d_ref[lo:, :] = jnp.where(keep, d_ref[lo:, :], 0.0) - upd[lo:]
    left_order = (0, 0, 1, 1, 0, 2)
    right_order = (0, 1, 0, 1, 2, 0)

    def left_of(parts):
        return jnp.concatenate([parts[i] for i in left_order], axis=1)

    def right_of(parts):
        return jnp.concatenate([parts[i] for i in right_order], axis=0)

    def panel(t, lo, hi):
        left = left_of([w3_ref[i] for i in range(3)])
        right = right_of(thirds(a_ref[t * B:(t + 1) * B, lo * B:hi * B]))
        p = jnp.dot(left, right, preferred_element_type=f32)
        if hi == nblk + 1:
            z_ref[t * B:(t + 1) * B, :] = p[:, -B:]
        if t + 1 == nblk:
            return
        for i, part in enumerate(thirds(p)):
            p3_ref[i, :, lo * B:hi * B] = part
        for c in range(lo, min(hi, nblk)):
            for i, part in enumerate(thirds(p[:, (c - lo) * B:(c - lo + 1) * B].T)):
                pt_ref[i, c * B:(c + 1) * B, :] = part

    def trailing(j, lo, hi):
        left = left_of([pt_ref[i, j * B:(j + 1) * B, :] for i in range(3)])
        right = right_of([p3_ref[i, :, lo * B:hi * B] for i in range(3)])
        return jnp.dot(left, right, preferred_element_type=f32)

    def update(j, lo, hi):
        a_ref[j * B:(j + 1) * B, lo * B:hi * B] = a_ref[j * B:(j + 1) * B, lo * B:hi * B] - trailing(j, lo, hi)

    build(0, (0,))
    d_ref[...] = a_ref[:B, :B]
    always = chol_id >= 0
    for k in range(nblk):
        for s in range(steps):
            @pl.when(always)
            def _(k=k, s=s):
                if s == 0:
                    begin(0, d_ref[0:8, :], d_ref[8:16, :], 0)
                if s and s + 1 < steps:
                    near2(s - 1)
                if s:
                    distant(s - 1)
                if k == 0:
                    if s < nblk:
                        build(s, range(max(s, 1), nblk))
                elif s == 0:
                    panel(k - 1, k + 1, nblk + 1)
                elif k + s - 1 < nblk:
                    j = k + s - 1
                    update(j, max(j, k + 1), nblk + 1)
                chain(s)
        for i, part in enumerate(thirds(jnp.where(lane <= sub, w_ref[...], 0.0))):
            w3_ref[i] = part
        if k == nc:
            m_ref[...] = -a_ref[cond:, total:]
        panel(k, k + 1, k + 2)
        if k + 1 < nblk:
            d_ref[...] = a_ref[(k + 1) * B:(k + 2) * B, (k + 1) * B:(k + 2) * B] - trailing(k + 1, k + 1, k + 2)

    out = mean_ref.shape[1]
    start = pl.multiple_of(chol_id * out, 8)
    pad = jnp.zeros((B - out, B), f32)
    mt = jnp.concatenate([m_ref[pl.ds(start, out), :], pad], axis=0).T
    zt = jnp.concatenate([z_ref[pl.ds(cond + start, out), :], pad], axis=0).T
    mean_ref[...] = mt[cols:2 * cols, :out]
    white_ref[...] = zt[:cols, :out]


def on_device(leaves, chols, coords, observed, cond_index):
    own = coords.shape[1]
    cond = cond_index.shape[1]
    cols = observed.shape[0]
    packed = jnp.concatenate([coords, observed], axis=0)
    out = own // chols
    total = own + cond
    bits = leaves.bit_length() - 1
    masks = tuple((1 << t) ^ (1 << (t - 1) if t > 1 else 0) for t in range(bits))
    grouped = 2 * cond // leaves % B == 0
    labels = [0]
    if grouped:
        pieces = [packed]
        def swap(even, odd):
            return [(j * chols + c, (j ^ (odd if c % 2 else even)) * chols + c)
                    for j in range(leaves) for c in range(chols) if (odd if c % 2 else even)]
        plan = [(m + (m >> 1 & 1), m + 1 - (m >> 1 & 1)) for m in range(0, leaves, 2)]
        got = [lax.ppermute(packed, ("leaf", "chol"), swap(*p)) for p in plan]
        cross = [(j, j ^ 1) for j in range(chols)]
        pieces += got + [lax.ppermute(g, "chol", cross) for g in got]
        labels = [0] + [p[0] + 256 * p[1] for p in plan] + [p[1] + 256 * p[0] for p in plan]
        rows = -(-packed.shape[0] // 8) * 8
    else:
        every = packed
        for mask in masks:
            swap = [(j, j ^ mask) for j in range(leaves)]
            every = jnp.concatenate([every, lax.ppermute(every, "leaf", swap)], axis=1)
        far = cond_index[0] // own ^ lax.axis_index("leaf")
        place = jnp.zeros_like(far)
        for bit in range(bits - 1, -1, -1):
            has = (far >> bit) & 1
            place = place + (has << bit)
            far = far ^ (has * masks[bit])
        pieces = [packed, jnp.take(every, place * own + cond_index[0] % own, axis=1)]
        rows = 8
    return pl.pallas_call(
        functools.partial(kernel, "leaf", "chol", tuple(labels) if grouped else ()),
        out_shape=(jax.ShapeDtypeStruct((cols, out), f32),) * 2,
        in_specs=[pl.BlockSpec(memory_space=pltpu.SMEM)]
        + [pl.BlockSpec(memory_space=pltpu.VMEM)] * (1 + len(pieces)),
        out_specs=(pl.BlockSpec(memory_space=pltpu.VMEM),) * 2,
        scratch_shapes=[
            pltpu.VMEM((total, total + B), f32),
            pltpu.VMEM((B, B), f32),
            pltpu.VMEM((2, 5, 8, 8, B), f32),
            pltpu.VMEM((2, 2, 8, B), f32),
            pltpu.VMEM((B, B), f32),
            pltpu.VMEM((total, B), f32),
            pltpu.VMEM((own, B), f32),
            pltpu.VMEM((leaves + 1 if grouped else 1, rows, own), f32),
            pltpu.VMEM((8, total), f32),
            pltpu.VMEM((3, B, B), bf16),
            pltpu.VMEM((3, B, total + B), bf16),
            pltpu.VMEM((3, total, B), bf16),
            pltpu.VMEM((8, 2, 8, B), f32),
        ],
        compiler_params=pltpu.CompilerParams(vmem_limit_bytes=48 << 20),
        name="vecchia",
    )(cond_index, cond_index, *pieces)


def solution(mesh):
    return jax.shard_map(
        functools.partial(on_device, mesh.shape["leaf"], mesh.shape["chol"]),
        mesh=mesh,
        in_specs=(P(None, "leaf"), P(None, "leaf"), P("leaf", None)),
        out_specs=(P(None, ("leaf", "chol")), P(None, ("leaf", "chol"))),
        check_vma=False,
    )
```

time: 42.1 us -> 36.8 us (0.87)
  Pallas kernels: 27.9 us -> 22.6 us
    pallas_call x1, Pallas kernels: 27.9 us -> 22.6 us  [on_device(): pl.pallas_call(functools.partial(kernel, 'leaf', 'chol', tuple(labels) if...]
where the time goes in v3:
time: 36.8 us; the launch traced here: 36.6 us
  Pallas kernels  22.6 us (61%)
  starting transfers between devices  8.02 us (22%)
  waiting for transfers between devices  4.59 us (12%)
  other arithmetic  0.75 us (2%)
  between operations  0.66 us (2%)
    pallas_call x1, Pallas kernels, on_device(): pl.pallas_call(functools.partial(kernel, 'leaf', 'chol', tuple(labels) if...  22.6 us
    ppermute x4, starting transfers between devices, on_device(): got = [lax.ppermute(packed, ('leaf', 'chol'), swap(*p)) for p in plan]  7.32 us
    ppermute x4, waiting for transfers between devices, on_device(): got = [lax.ppermute(packed, ('leaf', 'chol'), swap(*p)) for p in plan]  3.71 us
    ppermute x4, waiting for transfers between devices, on_device(): pieces += got + [lax.ppermute(g, 'chol', cross) for g in got]  0.88 us
    concatenate x1, other arithmetic, on_device(): packed = jnp.concatenate([coords, observed], axis=0)  0.75 us
  transfers between devices with their start and end apart: 8, of which 6 were waited for; matrix products, arithmetic and copies ran while one was open for 0% of the time, Pallas kernels for 0%

profile of v3, /device:TPU:0, one launch (start us, length us, event | category | flops | bytes accessed | tf_op | source)
XLA Modules:
  0.0 36.6 jit_solution(2204853096616064908)
XLA Ops:
  0.6 0.0 copy-start
  0.6 0.8 %pad_maximum_fusion.refs_0_ = f32[19,384]{1,0:T(8,128)S(1)} fusion(f32[16,384]{1,0:T(8,128)} %param.4, f32[3,384]{1,0:T(4,128)} %param.3), kind=kLoop, calls=%fused_computation | loop fusion | flops 7296 | bytes 58368 | tf_op jit(solution)/shard_map/concatenate | solution.py:279
  1.4 6.0 %collective-permute-start.3 = (f32[19,384]{1,0:T(8,128)S(1)}, f32[19,384]{1,0:T(8,128)S(1)}, u32[]{:S(2)}, u32[]{:S(2)}) collective-permute-start(f32[19,384]{1,0:T(8,128)S(1)} %pad_maximum_fusion.refs_0_), channel_id=1, source_target_pairs={{0,28},{1,25},{2,30},{3,27},{4,24},{5,29},{6,26},{7,31},{8,20},{9,... | collective-permute-start | bytes 87560 | tf_op jit(solution)/shard_map/ppermute | solution.py:292
  7.4 0.0 collective-permute-start.2
  7.4 0.6 %collective-permute-start.1 = (f32[19,384]{1,0:T(8,128)S(1)}, f32[19,384]{1,0:T(8,128)S(1)}, u32[]{:S(2)}, u32[]{:S(2)}) collective-permute-start(f32[19,384]{1,0:T(8,128)S(1)} %pad_maximum_fusion.refs_0_), channel_id=1, source_target_pairs={{0,12},{1,9},{2,14},{3,11},{4,8},{5,13},{6,10},{7,15},{8,4},{9,1},... | collective-permute-start | bytes 87560 | tf_op jit(solution)/shard_map/ppermute | solution.py:292
  8.1 0.7 %collective-permute-start = (f32[19,384]{1,0:T(8,128)S(1)}, f32[19,384]{1,0:T(8,128)S(1)}, u32[]{:S(2)}, u32[]{:S(2)}) collective-permute-start(f32[19,384]{1,0:T(8,128)S(1)} %pad_maximum_fusion.refs_0_), channel_id=1, source_target_pairs={{1,5},{3,7},{5,1},{7,3},{9,13},{11,15},{13,9},{15,11},{17,21},{19,... | collective-permute-start | bytes 87560 | tf_op jit(solution)/shard_map/ppermute | solution.py:292
  8.7 0.6 %collective-permute-done.3.refs_4_ = f32[19,384]{1,0:T(8,128)S(1)} collective-permute-done((f32[19,384]{1,0:T(8,128)S(1)}, f32[19,384]{1,0:T(8,128)S(1)}, u32[]{:S(2)}, u32[]{:S(2)}) %collective-permute-start.3) | collective-permute-done | bytes 29216 | tf_op jit(solution)/shard_map/ppermute | solution.py:292
  9.4 0.2 collective-permute-start.7
  9.5 2.7 %collective-permute-done.2.refs_3_ = f32[19,384]{1,0:T(8,128)S(1)} collective-permute-done((f32[19,384]{1,0:T(8,128)S(1)}, f32[19,384]{1,0:T(8,128)S(1)}, u32[]{:S(2)}, u32[]{:S(2)}) %collective-permute-start.2) | collective-permute-done | bytes 29216 | tf_op jit(solution)/shard_map/ppermute | solution.py:292
  12.3 0.0 collective-permute-start.6
  12.3 0.3 collective-permute-done.1.refs_2_
  12.6 0.2 collective-permute-start.5
  12.8 0.0 collective-permute-done.refs_1_
  12.8 0.3 collective-permute-start.4
  13.1 0.0 collective-permute-done.7.refs_8_
  13.1 0.4 collective-permute-done.6.refs_7_
  13.5 0.3 collective-permute-done.5.refs_6_
  13.8 0.2 collective-permute-done.4.refs_5_
  14.0 0.0 copy-done
  14.0 22.6 %vecchia.1 = (f32[16,96]{1,0:T(8,128)}, f32[16,96]{1,0:T(8,128)}) custom-call(s32[1,512]{1,0:T(1,128)S(1)} %copy-done, s32[1,512]{1,0:T(1,128)S(1)} %copy-done, f32[19,384]{1,0:T(8,128)S(1)} %pad_maximum_fusion.refs_0_, f32[19,384]{1,0:T(8,128)S(1)} %collective-permute-done.refs_1_, f32[19,384]{1,0:T(8,128)S(1)} %collective-permute-done.1.refs_2_, ...), custom_call_target="tpu_custom_call" | custom-call | tf_op jit(solution)/shard_map/vecchia/pallas_call | solution.py:310
Async XLA Ops:
  0.6 13.4 %copy-start = (s32[1,512]{1,0:T(1,128)S(1)}, s32[1,512]{1,0:T(1,128)}, u32[]{:S(2)}) copy-start(s32[1,512]{1,0:T(1,128)} %idx_ref.1) | copy-start | bytes 6148
  1.4 8.0 %collective-permute-start.3 = (f32[19,384]{1,0:T(8,128)S(1)}, f32[19,384]{1,0:T(8,128)S(1)}, u32[]{:S(2)}, u32[]{:S(2)}) collective-permute-start(f32[19,384]{1,0:T(8,128)S(1)} %pad_maximum_fusion.refs_0_), channel_id=1, source_target_pairs={{0,28},{1,25},{2,30},{3,27},{4,24},{5,29},{6,26},{7,31},{8,20},{9,... | collective-permute-start | bytes 87560 | tf_op jit(solution)/shard_map/ppermute | solution.py:292
  7.4 4.9 %collective-permute-start.2 = (f32[19,384]{1,0:T(8,128)S(1)}, f32[19,384]{1,0:T(8,128)S(1)}, u32[]{:S(2)}, u32[]{:S(2)}) collective-permute-start(f32[19,384]{1,0:T(8,128)S(1)} %pad_maximum_fusion.refs_0_), channel_id=1, source_target_pairs={{0,16},{1,21},{2,18},{3,23},{4,20},{5,17},{6,22},{7,19},{8,24},{9,... | collective-permute-start | bytes 87560 | tf_op jit(solution)/shard_map/ppermute | solution.py:292
  7.4 5.2 %collective-permute-start.1 = (f32[19,384]{1,0:T(8,128)S(1)}, f32[19,384]{1,0:T(8,128)S(1)}, u32[]{:S(2)}, u32[]{:S(2)}) collective-permute-start(f32[19,384]{1,0:T(8,128)S(1)} %pad_maximum_fusion.refs_0_), channel_id=1, source_target_pairs={{0,12},{1,9},{2,14},{3,11},{4,8},{5,13},{6,10},{7,15},{8,4},{9,1},... | collective-permute-start | bytes 87560 | tf_op jit(solution)/shard_map/ppermute | solution.py:292
  8.1 4.7 %collective-permute-start = (f32[19,384]{1,0:T(8,128)S(1)}, f32[19,384]{1,0:T(8,128)S(1)}, u32[]{:S(2)}, u32[]{:S(2)}) collective-permute-start(f32[19,384]{1,0:T(8,128)S(1)} %pad_maximum_fusion.refs_0_), channel_id=1, source_target_pairs={{1,5},{3,7},{5,1},{7,3},{9,13},{11,15},{13,9},{15,11},{17,21},{19,... | collective-permute-start | bytes 87560 | tf_op jit(solution)/shard_map/ppermute | solution.py:292
  9.4 3.8 %collective-permute-start.7 = (f32[19,384]{1,0:T(8,128)S(1)}, f32[19,384]{1,0:T(8,128)S(1)}, u32[]{:S(2)}, u32[]{:S(2)}) collective-permute-start(f32[19,384]{1,0:T(8,128)S(1)} %collective-permute-done.3.refs_4_), channel_id=1, source_target_pairs={{0,1},{1,0},{2,3},{3,2},{4,5},{5,4},{6,7},{7,6},{8,9},{9,8},{10,11... | collective-permute-start | bytes 87560 | tf_op jit(solution)/shard_map/ppermute | solution.py:294
  12.3 1.2 %collective-permute-start.6 = (f32[19,384]{1,0:T(8,128)S(1)}, f32[19,384]{1,0:T(8,128)S(1)}, u32[]{:S(2)}, u32[]{:S(2)}) collective-permute-start(f32[19,384]{1,0:T(8,128)S(1)} %collective-permute-done.2.refs_3_), channel_id=1, source_target_pairs={{0,1},{1,0},{2,3},{3,2},{4,5},{5,4},{6,7},{7,6},{8,9},{9,8},{10,11... | collective-permute-start | bytes 87560 | tf_op jit(solution)/shard_map/ppermute | solution.py:294
  12.6 1.2 %collective-permute-start.5 = (f32[19,384]{1,0:T(8,128)S(1)}, f32[19,384]{1,0:T(8,128)S(1)}, u32[]{:S(2)}, u32[]{:S(2)}) collective-permute-start(f32[19,384]{1,0:T(8,128)S(1)} %collective-permute-done.1.refs_2_), channel_id=1, source_target_pairs={{0,1},{1,0},{2,3},{3,2},{4,5},{5,4},{6,7},{7,6},{8,9},{9,8},{10,11... | collective-permute-start | bytes 87560 | tf_op jit(solution)/shard_map/ppermute | solution.py:294
  12.8 1.2 %collective-permute-start.4 = (f32[19,384]{1,0:T(8,128)S(1)}, f32[19,384]{1,0:T(8,128)S(1)}, u32[]{:S(2)}, u32[]{:S(2)}) collective-permute-start(f32[19,384]{1,0:T(8,128)S(1)} %collective-permute-done.refs_1_), channel_id=1, source_target_pairs={{0,1},{1,0},{2,3},{3,2},{4,5},{5,4},{6,7},{7,6},{8,9},{9,8},{10,11... | collective-permute-start | bytes 87560 | tf_op jit(solution)/shard_map/ppermute | solution.py:294

commit v4 on v3

--- a/solution.py
+++ b/solution.py
@@ -23,10 +23,10 @@
 
 
 def kernel(leaf_axis, chol_axis, masks, pos_ref, idx_ref, *refs):
-    npieces = len(refs) - 15
+    npieces = len(refs) - 16
     piece_refs = refs[:npieces]
     (mean_ref, white_ref, a_ref, d_ref, v_ref, x_ref, w_ref, z_ref, m_ref,
-     g_ref, f_ref, w3_ref, p3_ref, pt_ref, n_ref) = refs[npieces:]
+     g_ref, f_ref, w3_ref, p3_ref, pt_ref, n_ref, q_ref) = refs[npieces:]
     own_ref = piece_refs[0]
     own = own_ref.shape[1]
     cond = idx_ref.shape[1]
@@ -69,28 +69,31 @@
             alive = (idx_ref[:, k * B:(k + 1) * B] // own != leaf_id).astype(f32)
             vals = blk[3:] * alive
             vals2 = vals
+            away = (lax.broadcasted_iota(jnp.int32, (1, B), 1) + (k * B + 2)).astype(f32) * 1e3
+            pts = jnp.where(alive > 0.5, blk[:3], away)
         else:
             blk = own_ref[:, (k - nc) * B:(k - nc + 1) * B]
             alive = jnp.ones((1, B), f32)
             vals = blk[3:]
             vals2 = jnp.zeros_like(vals)
+            pts = blk[:3]
         stack = jnp.concatenate(
-            [vals, vals2, blk[:3], alive, jnp.zeros((B - c0 - 4, B), f32)], axis=0)
+            [vals, vals2, pts, jnp.zeros((B - c0 - 3, B), f32)], axis=0)
         t = stack.T
-        f_ref[:, k * B:(k + 1) * B] = jnp.concatenate([blk[:3], alive, jnp.zeros((4, B), f32)], axis=0)
-        a_ref[k * B:(k + 1) * B, total:] = t
+        f_ref[:, k * B:(k + 1) * B] = jnp.concatenate([pts, alive, jnp.zeros((4, B), f32)], axis=0)
+        a_ref[k * B:(k + 1) * B, total:] = jnp.where(lane < c0, t, 0.0)
+        q_ref[k * B:(k + 1) * B, :] = t
 
     def build(k, tiles):
-        t = a_ref[k * B:(k + 1) * B, total:]
-        cx, cy, cz, ca = (jnp.broadcast_to(t[:, c0 + i:c0 + i + 1], (B, B)) for i in range(4))
+        t = q_ref[k * B:(k + 1) * B, :]
+        cx, cy, cz = (jnp.broadcast_to(t[:, c0 + i:c0 + i + 1], (B, B)) for i in range(3))
         for c in tiles:
             rx, ry, rz, ra = (f_ref[i:i + 1, c * B:(c + 1) * B] for i in range(4))
             dx, dy, dz = cx - rx, cy - ry, cz - rz
             sq = jnp.maximum(dx * dx + dy * dy + dz * dz, 1e-30)
-            dist = sq * lax.rsqrt(sq)
-            kern = jnp.exp(dist * (-1.0 / length_scale)) * (ca * ra)
+            kern = jnp.exp2(sq * lax.rsqrt(sq) * (-1.4426950408889634 / length_scale))
             if c == k:
-                kern = jnp.where(lane == sub, kern + (nugget * ra + 1.0 - ra), kern)
+                kern = jnp.where(lane == sub, kern + nugget * ra, kern)
             a_ref[k * B:(k + 1) * B, c * B:(c + 1) * B] = kern
 
     lane8 = lax.broadcasted_iota(jnp.int32, (8, B), 1)
@@ -327,6 +330,7 @@
             pltpu.VMEM((3, B, total + B), bf16),
             pltpu.VMEM((3, total, B), bf16),
             pltpu.VMEM((8, 2, 8, B), f32),
+            pltpu.VMEM((total, B), f32),
         ],
         compiler_params=pltpu.CompilerParams(vmem_limit_bytes=48 << 20),
         name="vecchia",

time: 36.8 us -> 36.5 us (level)
  no operation moved by 1% of the time
where the time goes in v4:
time: 36.5 us; the launch traced here: 36.3 us
  Pallas kernels  22.3 us (61%)
  starting transfers between devices  8.02 us (22%)
  waiting for transfers between devices  4.59 us (13%)
  other arithmetic  0.75 us (2%)
  between operations  0.66 us (2%)
    pallas_call x1, Pallas kernels, on_device(): pl.pallas_call(functools.partial(kernel, 'leaf', 'chol', tuple(labels) if...  22.3 us
    ppermute x4, starting transfers between devices, on_device(): got = [lax.ppermute(packed, ('leaf', 'chol'), swap(*p)) for p in plan]  7.32 us
    ppermute x4, waiting for transfers between devices, on_device(): got = [lax.ppermute(packed, ('leaf', 'chol'), swap(*p)) for p in plan]  3.71 us
    ppermute x4, waiting for transfers between devices, on_device(): pieces += got + [lax.ppermute(g, 'chol', cross) for g in got]  0.88 us
    concatenate x1, other arithmetic, on_device(): packed = jnp.concatenate([coords, observed], axis=0)  0.75 us
  transfers between devices with their start and end apart: 8, of which 6 were waited for; matrix products, arithmetic and copies ran while one was open for 0% of the time, Pallas kernels for 0%

profile of v4, /device:TPU:0, one launch (start us, length us, event | category | flops | bytes accessed | tf_op | source)
XLA Modules:
  0.0 36.3 jit_solution(13581688925252764785)
XLA Ops:
  0.6 0.0 copy-start
  0.6 0.8 %pad_maximum_fusion.refs_0_ = f32[19,384]{1,0:T(8,128)S(1)} fusion(f32[16,384]{1,0:T(8,128)} %param.4, f32[3,384]{1,0:T(4,128)} %param.3), kind=kLoop, calls=%fused_computation | loop fusion | flops 7296 | bytes 58368 | tf_op jit(solution)/shard_map/concatenate | solution.py:282
  1.4 6.0 %collective-permute-start.3 = (f32[19,384]{1,0:T(8,128)S(1)}, f32[19,384]{1,0:T(8,128)S(1)}, u32[]{:S(2)}, u32[]{:S(2)}) collective-permute-start(f32[19,384]{1,0:T(8,128)S(1)} %pad_maximum_fusion.refs_0_), channel_id=1, source_target_pairs={{0,28},{1,25},{2,30},{3,27},{4,24},{5,29},{6,26},{7,31},{8,20},{9,... | collective-permute-start | bytes 87560 | tf_op jit(solution)/shard_map/ppermute | solution.py:295
  7.4 0.0 collective-permute-start.2
  7.4 0.6 %collective-permute-start.1 = (f32[19,384]{1,0:T(8,128)S(1)}, f32[19,384]{1,0:T(8,128)S(1)}, u32[]{:S(2)}, u32[]{:S(2)}) collective-permute-start(f32[19,384]{1,0:T(8,128)S(1)} %pad_maximum_fusion.refs_0_), channel_id=1, source_target_pairs={{0,12},{1,9},{2,14},{3,11},{4,8},{5,13},{6,10},{7,15},{8,4},{9,1},... | collective-permute-start | bytes 87560 | tf_op jit(solution)/shard_map/ppermute | solution.py:295
  8.1 0.7 %collective-permute-start = (f32[19,384]{1,0:T(8,128)S(1)}, f32[19,384]{1,0:T(8,128)S(1)}, u32[]{:S(2)}, u32[]{:S(2)}) collective-permute-start(f32[19,384]{1,0:T(8,128)S(1)} %pad_maximum_fusion.refs_0_), channel_id=1, source_target_pairs={{1,5},{3,7},{5,1},{7,3},{9,13},{11,15},{13,9},{15,11},{17,21},{19,... | collective-permute-start | bytes 87560 | tf_op jit(solution)/shard_map/ppermute | solution.py:295
  8.7 0.6 %collective-permute-done.3.refs_4_ = f32[19,384]{1,0:T(8,128)S(1)} collective-permute-done((f32[19,384]{1,0:T(8,128)S(1)}, f32[19,384]{1,0:T(8,128)S(1)}, u32[]{:S(2)}, u32[]{:S(2)}) %collective-permute-start.3) | collective-permute-done | bytes 29216 | tf_op jit(solution)/shard_map/ppermute | solution.py:295
  9.4 0.2 collective-permute-start.7
  9.5 2.7 %collective-permute-done.2.refs_3_ = f32[19,384]{1,0:T(8,128)S(1)} collective-permute-done((f32[19,384]{1,0:T(8,128)S(1)}, f32[19,384]{1,0:T(8,128)S(1)}, u32[]{:S(2)}, u32[]{:S(2)}) %collective-permute-start.2) | collective-permute-done | bytes 29216 | tf_op jit(solution)/shard_map/ppermute | solution.py:295
  12.3 0.0 collective-permute-start.6
  12.3 0.3 collective-permute-done.1.refs_2_
  12.6 0.2 collective-permute-start.5
  12.8 0.0 collective-permute-done.refs_1_
  12.8 0.3 collective-permute-start.4
  13.1 0.0 collective-permute-done.7.refs_8_
  13.1 0.4 collective-permute-done.6.refs_7_
  13.5 0.3 collective-permute-done.5.refs_6_
  13.8 0.2 collective-permute-done.4.refs_5_
  14.0 0.0 copy-done
  14.0 22.3 %vecchia.1 = (f32[16,96]{1,0:T(8,128)}, f32[16,96]{1,0:T(8,128)}) custom-call(s32[1,512]{1,0:T(1,128)S(1)} %copy-done, s32[1,512]{1,0:T(1,128)S(1)} %copy-done, f32[19,384]{1,0:T(8,128)S(1)} %pad_maximum_fusion.refs_0_, f32[19,384]{1,0:T(8,128)S(1)} %collective-permute-done.refs_1_, f32[19,384]{1,0:T(8,128)S(1)} %collective-permute-done.1.refs_2_, ...), custom_call_target="tpu_custom_call" | custom-call | tf_op jit(solution)/shard_map/vecchia/pallas_call | solution.py:313
Async XLA Ops:
  0.6 13.4 %copy-start = (s32[1,512]{1,0:T(1,128)S(1)}, s32[1,512]{1,0:T(1,128)}, u32[]{:S(2)}) copy-start(s32[1,512]{1,0:T(1,128)} %idx_ref.1) | copy-start | bytes 6148
  1.4 8.0 %collective-permute-start.3 = (f32[19,384]{1,0:T(8,128)S(1)}, f32[19,384]{1,0:T(8,128)S(1)}, u32[]{:S(2)}, u32[]{:S(2)}) collective-permute-start(f32[19,384]{1,0:T(8,128)S(1)} %pad_maximum_fusion.refs_0_), channel_id=1, source_target_pairs={{0,28},{1,25},{2,30},{3,27},{4,24},{5,29},{6,26},{7,31},{8,20},{9,... | collective-permute-start | bytes 87560 | tf_op jit(solution)/shard_map/ppermute | solution.py:295
  7.4 4.9 %collective-permute-start.2 = (f32[19,384]{1,0:T(8,128)S(1)}, f32[19,384]{1,0:T(8,128)S(1)}, u32[]{:S(2)}, u32[]{:S(2)}) collective-permute-start(f32[19,384]{1,0:T(8,128)S(1)} %pad_maximum_fusion.refs_0_), channel_id=1, source_target_pairs={{0,16},{1,21},{2,18},{3,23},{4,20},{5,17},{6,22},{7,19},{8,24},{9,... | collective-permute-start | bytes 87560 | tf_op jit(solution)/shard_map/ppermute | solution.py:295
  7.4 5.2 %collective-permute-start.1 = (f32[19,384]{1,0:T(8,128)S(1)}, f32[19,384]{1,0:T(8,128)S(1)}, u32[]{:S(2)}, u32[]{:S(2)}) collective-permute-start(f32[19,384]{1,0:T(8,128)S(1)} %pad_maximum_fusion.refs_0_), channel_id=1, source_target_pairs={{0,12},{1,9},{2,14},{3,11},{4,8},{5,13},{6,10},{7,15},{8,4},{9,1},... | collective-permute-start | bytes 87560 | tf_op jit(solution)/shard_map/ppermute | solution.py:295
  8.1 4.7 %collective-permute-start = (f32[19,384]{1,0:T(8,128)S(1)}, f32[19,384]{1,0:T(8,128)S(1)}, u32[]{:S(2)}, u32[]{:S(2)}) collective-permute-start(f32[19,384]{1,0:T(8,128)S(1)} %pad_maximum_fusion.refs_0_), channel_id=1, source_target_pairs={{1,5},{3,7},{5,1},{7,3},{9,13},{11,15},{13,9},{15,11},{17,21},{19,... | collective-permute-start | bytes 87560 | tf_op jit(solution)/shard_map/ppermute | solution.py:295
  9.4 3.8 %collective-permute-start.7 = (f32[19,384]{1,0:T(8,128)S(1)}, f32[19,384]{1,0:T(8,128)S(1)}, u32[]{:S(2)}, u32[]{:S(2)}) collective-permute-start(f32[19,384]{1,0:T(8,128)S(1)} %collective-permute-done.3.refs_4_), channel_id=1, source_target_pairs={{0,1},{1,0},{2,3},{3,2},{4,5},{5,4},{6,7},{7,6},{8,9},{9,8},{10,11... | collective-permute-start | bytes 87560 | tf_op jit(solution)/shard_map/ppermute | solution.py:297
  12.3 1.2 %collective-permute-start.6 = (f32[19,384]{1,0:T(8,128)S(1)}, f32[19,384]{1,0:T(8,128)S(1)}, u32[]{:S(2)}, u32[]{:S(2)}) collective-permute-start(f32[19,384]{1,0:T(8,128)S(1)} %collective-permute-done.2.refs_3_), channel_id=1, source_target_pairs={{0,1},{1,0},{2,3},{3,2},{4,5},{5,4},{6,7},{7,6},{8,9},{9,8},{10,11... | collective-permute-start | bytes 87560 | tf_op jit(solution)/shard_map/ppermute | solution.py:297
  12.6 1.2 %collective-permute-start.5 = (f32[19,384]{1,0:T(8,128)S(1)}, f32[19,384]{1,0:T(8,128)S(1)}, u32[]{:S(2)}, u32[]{:S(2)}) collective-permute-start(f32[19,384]{1,0:T(8,128)S(1)} %collective-permute-done.1.refs_2_), channel_id=1, source_target_pairs={{0,1},{1,0},{2,3},{3,2},{4,5},{5,4},{6,7},{7,6},{8,9},{9,8},{10,11... | collective-permute-start | bytes 87560 | tf_op jit(solution)/shard_map/ppermute | solution.py:297
  12.8 1.2 %collective-permute-start.4 = (f32[19,384]{1,0:T(8,128)S(1)}, f32[19,384]{1,0:T(8,128)S(1)}, u32[]{:S(2)}, u32[]{:S(2)}) collective-permute-start(f32[19,384]{1,0:T(8,128)S(1)} %collective-permute-done.refs_1_), channel_id=1, source_target_pairs={{0,1},{1,0},{2,3},{3,2},{4,5},{5,4},{6,7},{7,6},{8,9},{9,8},{10,11... | collective-permute-start | bytes 87560 | tf_op jit(solution)/shard_map/ppermute | solution.py:297

commit v5 on v4

--- a/solution.py
+++ b/solution.py
@@ -238,11 +238,9 @@
 
     build(0, (0,))
     d_ref[...] = a_ref[:B, :B]
-    always = chol_id >= 0
     for k in range(nblk):
         for s in range(steps):
-            @pl.when(always)
-            def _(k=k, s=s):
+            with jax.named_scope("step"):
                 if s == 0:
                     begin(0, d_ref[0:8, :], d_ref[8:16, :], 0)
                 if s and s + 1 < steps:

time: 36.5 us -> 35.6 us (0.975)
  Pallas kernels: 22.3 us -> 21.4 us
    pallas_call x1, Pallas kernels: 22.3 us -> 21.4 us  [on_device(): pl.pallas_call(functools.partial(kernel, 'leaf', 'chol', tuple(labels) if...]
where the time goes in v5:
time: 35.6 us; the launch traced here: 35.5 us
  Pallas kernels  21.4 us (60%)
  starting transfers between devices  8.02 us (23%)
  waiting for transfers between devices  4.59 us (13%)
  other arithmetic  0.75 us (2%)
  between operations  0.66 us (2%)
    pallas_call x1, Pallas kernels, on_device(): pl.pallas_call(functools.partial(kernel, 'leaf', 'chol', tuple(labels) if...  21.4 us
    ppermute x4, starting transfers between devices, on_device(): got = [lax.ppermute(packed, ('leaf', 'chol'), swap(*p)) for p in plan]  7.32 us
    ppermute x4, waiting for transfers between devices, on_device(): got = [lax.ppermute(packed, ('leaf', 'chol'), swap(*p)) for p in plan]  3.71 us
    ppermute x4, waiting for transfers between devices, on_device(): pieces += got + [lax.ppermute(g, 'chol', cross) for g in got]  0.88 us
    concatenate x1, other arithmetic, on_device(): packed = jnp.concatenate([coords, observed], axis=0)  0.75 us
  transfers between devices with their start and end apart: 8, of which 6 were waited for; matrix products, arithmetic and copies ran while one was open for 0% of the time, Pallas kernels for 0%

profile of v5, /device:TPU:0, one launch (start us, length us, event | category | flops | bytes accessed | tf_op | source)
XLA Modules:
  0.0 35.5 jit_solution(7816407465311240913)
XLA Ops:
  0.6 0.0 copy-start
  0.6 0.8 %pad_maximum_fusion.refs_0_ = f32[19,384]{1,0:T(8,128)S(1)} fusion(f32[16,384]{1,0:T(8,128)} %param.4, f32[3,384]{1,0:T(4,128)} %param.3), kind=kLoop, calls=%fused_computation | loop fusion | flops 7296 | bytes 58368 | tf_op jit(solution)/shard_map/concatenate | solution.py:280
  1.4 6.0 %collective-permute-start.3 = (f32[19,384]{1,0:T(8,128)S(1)}, f32[19,384]{1,0:T(8,128)S(1)}, u32[]{:S(2)}, u32[]{:S(2)}) collective-permute-start(f32[19,384]{1,0:T(8,128)S(1)} %pad_maximum_fusion.refs_0_), channel_id=1, source_target_pairs={{0,28},{1,25},{2,30},{3,27},{4,24},{5,29},{6,26},{7,31},{8,20},{9,... | collective-permute-start | bytes 87560 | tf_op jit(solution)/shard_map/ppermute | solution.py:293
  7.4 0.0 collective-permute-start.2
  7.4 0.6 %collective-permute-start.1 = (f32[19,384]{1,0:T(8,128)S(1)}, f32[19,384]{1,0:T(8,128)S(1)}, u32[]{:S(2)}, u32[]{:S(2)}) collective-permute-start(f32[19,384]{1,0:T(8,128)S(1)} %pad_maximum_fusion.refs_0_), channel_id=1, source_target_pairs={{0,12},{1,9},{2,14},{3,11},{4,8},{5,13},{6,10},{7,15},{8,4},{9,1},... | collective-permute-start | bytes 87560 | tf_op jit(solution)/shard_map/ppermute | solution.py:293
  8.1 0.7 %collective-permute-start = (f32[19,384]{1,0:T(8,128)S(1)}, f32[19,384]{1,0:T(8,128)S(1)}, u32[]{:S(2)}, u32[]{:S(2)}) collective-permute-start(f32[19,384]{1,0:T(8,128)S(1)} %pad_maximum_fusion.refs_0_), channel_id=1, source_target_pairs={{1,5},{3,7},{5,1},{7,3},{9,13},{11,15},{13,9},{15,11},{17,21},{19,... | collective-permute-start | bytes 87560 | tf_op jit(solution)/shard_map/ppermute | solution.py:293
  8.7 0.6 %collective-permute-done.3.refs_4_ = f32[19,384]{1,0:T(8,128)S(1)} collective-permute-done((f32[19,384]{1,0:T(8,128)S(1)}, f32[19,384]{1,0:T(8,128)S(1)}, u32[]{:S(2)}, u32[]{:S(2)}) %collective-permute-start.3) | collective-permute-done | bytes 29216 | tf_op jit(solution)/shard_map/ppermute | solution.py:293
  9.4 0.2 collective-permute-start.7
  9.5 2.7 %collective-permute-done.2.refs_3_ = f32[19,384]{1,0:T(8,128)S(1)} collective-permute-done((f32[19,384]{1,0:T(8,128)S(1)}, f32[19,384]{1,0:T(8,128)S(1)}, u32[]{:S(2)}, u32[]{:S(2)}) %collective-permute-start.2) | collective-permute-done | bytes 29216 | tf_op jit(solution)/shard_map/ppermute | solution.py:293
  12.3 0.0 collective-permute-start.6
  12.3 0.3 collective-permute-done.1.refs_2_
  12.6 0.2 collective-permute-start.5
  12.8 0.0 collective-permute-done.refs_1_
  12.8 0.3 collective-permute-start.4
  13.1 0.0 collective-permute-done.7.refs_8_
  13.1 0.4 %collective-permute-done.6.refs_7_ = f32[19,384]{1,0:T(8,128)S(1)} collective-permute-done((f32[19,384]{1,0:T(8,128)S(1)}, f32[19,384]{1,0:T(8,128)S(1)}, u32[]{:S(2)}, u32[]{:S(2)}) %collective-permute-start.6) | collective-permute-done | bytes 29216 | tf_op jit(solution)/shard_map/ppermute | solution.py:295
  13.5 0.3 collective-permute-done.5.refs_6_
  13.8 0.2 collective-permute-done.4.refs_5_
  14.0 0.0 copy-done
  14.0 21.4 %vecchia.1 = (f32[16,96]{1,0:T(8,128)}, f32[16,96]{1,0:T(8,128)}) custom-call(s32[1,512]{1,0:T(1,128)S(1)} %copy-done, s32[1,512]{1,0:T(1,128)S(1)} %copy-done, f32[19,384]{1,0:T(8,128)S(1)} %pad_maximum_fusion.refs_0_, f32[19,384]{1,0:T(8,128)S(1)} %collective-permute-done.refs_1_, f32[19,384]{1,0:T(8,128)S(1)} %collective-permute-done.1.refs_2_, ...), custom_call_target="tpu_custom_call" | custom-call | tf_op jit(solution)/shard_map/vecchia/pallas_call | solution.py:311
Async XLA Ops:
  0.6 13.4 %copy-start = (s32[1,512]{1,0:T(1,128)S(1)}, s32[1,512]{1,0:T(1,128)}, u32[]{:S(2)}) copy-start(s32[1,512]{1,0:T(1,128)} %idx_ref.1) | copy-start | bytes 6148
  1.4 8.0 %collective-permute-start.3 = (f32[19,384]{1,0:T(8,128)S(1)}, f32[19,384]{1,0:T(8,128)S(1)}, u32[]{:S(2)}, u32[]{:S(2)}) collective-permute-start(f32[19,384]{1,0:T(8,128)S(1)} %pad_maximum_fusion.refs_0_), channel_id=1, source_target_pairs={{0,28},{1,25},{2,30},{3,27},{4,24},{5,29},{6,26},{7,31},{8,20},{9,... | collective-permute-start | bytes 87560 | tf_op jit(solution)/shard_map/ppermute | solution.py:293
  7.4 4.9 %collective-permute-start.2 = (f32[19,384]{1,0:T(8,128)S(1)}, f32[19,384]{1,0:T(8,128)S(1)}, u32[]{:S(2)}, u32[]{:S(2)}) collective-permute-start(f32[19,384]{1,0:T(8,128)S(1)} %pad_maximum_fusion.refs_0_), channel_id=1, source_target_pairs={{0,16},{1,21},{2,18},{3,23},{4,20},{5,17},{6,22},{7,19},{8,24},{9,... | collective-permute-start | bytes 87560 | tf_op jit(solution)/shard_map/ppermute | solution.py:293
  7.4 5.2 %collective-permute-start.1 = (f32[19,384]{1,0:T(8,128)S(1)}, f32[19,384]{1,0:T(8,128)S(1)}, u32[]{:S(2)}, u32[]{:S(2)}) collective-permute-start(f32[19,384]{1,0:T(8,128)S(1)} %pad_maximum_fusion.refs_0_), channel_id=1, source_target_pairs={{0,12},{1,9},{2,14},{3,11},{4,8},{5,13},{6,10},{7,15},{8,4},{9,1},... | collective-permute-start | bytes 87560 | tf_op jit(solution)/shard_map/ppermute | solution.py:293
  8.1 4.7 %collective-permute-start = (f32[19,384]{1,0:T(8,128)S(1)}, f32[19,384]{1,0:T(8,128)S(1)}, u32[]{:S(2)}, u32[]{:S(2)}) collective-permute-start(f32[19,384]{1,0:T(8,128)S(1)} %pad_maximum_fusion.refs_0_), channel_id=1, source_target_pairs={{1,5},{3,7},{5,1},{7,3},{9,13},{11,15},{13,9},{15,11},{17,21},{19,... | collective-permute-start | bytes 87560 | tf_op jit(solution)/shard_map/ppermute | solution.py:293
  9.4 3.8 %collective-permute-start.7 = (f32[19,384]{1,0:T(8,128)S(1)}, f32[19,384]{1,0:T(8,128)S(1)}, u32[]{:S(2)}, u32[]{:S(2)}) collective-permute-start(f32[19,384]{1,0:T(8,128)S(1)} %collective-permute-done.3.refs_4_), channel_id=1, source_target_pairs={{0,1},{1,0},{2,3},{3,2},{4,5},{5,4},{6,7},{7,6},{8,9},{9,8},{10,11... | collective-permute-start | bytes 87560 | tf_op jit(solution)/shard_map/ppermute | solution.py:295
  12.3 1.2 %collective-permute-start.6 = (f32[19,384]{1,0:T(8,128)S(1)}, f32[19,384]{1,0:T(8,128)S(1)}, u32[]{:S(2)}, u32[]{:S(2)}) collective-permute-start(f32[19,384]{1,0:T(8,128)S(1)} %collective-permute-done.2.refs_3_), channel_id=1, source_target_pairs={{0,1},{1,0},{2,3},{3,2},{4,5},{5,4},{6,7},{7,6},{8,9},{9,8},{10,11... | collective-permute-start | bytes 87560 | tf_op jit(solution)/shard_map/ppermute | solution.py:295
  12.6 1.2 %collective-permute-start.5 = (f32[19,384]{1,0:T(8,128)S(1)}, f32[19,384]{1,0:T(8,128)S(1)}, u32[]{:S(2)}, u32[]{:S(2)}) collective-permute-start(f32[19,384]{1,0:T(8,128)S(1)} %collective-permute-done.1.refs_2_), channel_id=1, source_target_pairs={{0,1},{1,0},{2,3},{3,2},{4,5},{5,4},{6,7},{7,6},{8,9},{9,8},{10,11... | collective-permute-start | bytes 87560 | tf_op jit(solution)/shard_map/ppermute | solution.py:295
  12.8 1.2 %collective-permute-start.4 = (f32[19,384]{1,0:T(8,128)S(1)}, f32[19,384]{1,0:T(8,128)S(1)}, u32[]{:S(2)}, u32[]{:S(2)}) collective-permute-start(f32[19,384]{1,0:T(8,128)S(1)} %collective-permute-done.refs_1_), channel_id=1, source_target_pairs={{0,1},{1,0},{2,3},{3,2},{4,5},{5,4},{6,7},{7,6},{8,9},{9,8},{10,11... | collective-permute-start | bytes 87560 | tf_op jit(solution)/shard_map/ppermute | solution.py:295
